TPU v7x, 128 devices: a whole 4x4x4 slice. The times are simulated.
128 devices in a mesh: group: 8 (over z, x_lo), tensor: 16 (over y, x_hi, core).
Axes of the slice: x: 4 (x_hi: 2, x_lo: 2; x = x_hi * 2 + x_lo), y: 4, z: 4, core: 2. Of those that a mesh axis runs over, the one named last changes fastest.
Arguments:
- low_state: bfloat16 [4096, 8192], P('group', 'tensor'), may hold values from -6 to 6
- mid_state: bfloat16 [4096, 8192], P('group', 'tensor'), may hold values from -6 to 6
- residual: bfloat16 [4096, 8192], P('group', 'tensor'), may hold values from -6 to 6
- attention: bfloat16 [4096, 8192], P('group', 'tensor'), may hold values from -6 to 6
- o_weight: bfloat16 [8192, 8192], P('tensor'), may hold values from -0.0625 to 0.0625
- fc_weight: bfloat16 [3, 8192, 8192], P(None, 'tensor', 'group'), may hold values from -0.0390625 to 0.0390625
- norm_gain: float32 [8192], P('group'), may hold values from 0.1 to 1.9
- target: bfloat16 [2048, 8192], P('tensor', 'group'), may hold values from -6 to 6
- counts: int32 [8], replicated, may hold values from 32 to 256, as said below
- accept_rows: int32 [8, 512], replicated, may hold values from 0 to 511, each once within a row
- owners: int32 [8, 512], replicated, may hold values from 0 to 7, as said below
Outputs:
- top_state: bfloat16 [4096, 8192], P('group', 'tensor')
- fc_grad: float32 [3, 8192, 8192], P(None, 'tensor', 'group')
Inputs may be any that keep to these rules, and one draw needn't show every extreme that they name: The counts sum to exactly 1024. Every replica accepts at least 32 rows, and in every draw one replica accepts 8 * 32. `accept_rows`: only the first counts[g] entries of row g are accepted rows. `owners`: among the first counts[g] entries of row g no shard appears more than 32 times; in every draw one shard receives exactly 32 rows from every replica, and the replica with the most accepted rows sends 32 to every shard. Later entries are unused.
All inputs are finite; a program needn't handle non-finite values.
Results may differ from a plain program's by a relative error of at most 0.012.
Values may be sent and summed in bfloat16 or wider, within the bound.
A program may use at most 128 MiB of HBM per device.

v0:
```python
import jax
import jax.numpy as jnp
from jax import lax
from jax.sharding import PartitionSpec as P

D = 8192
SLOTS = 32


epsilon = 1e-05


def send_plan(counts, accept_rows, owners, group_count, group_index, slots):
    rows = owners.shape[1]
    live = jnp.arange(rows, dtype=jnp.int32)[None, :] < counts[:, None]
    onehot = (
        (owners[:, :, None] == jnp.arange(group_count, dtype=jnp.int32)[None, None, :])
        & live[:, :, None]
    ).astype(jnp.int32)
    mine = lax.dynamic_index_in_dim(onehot, group_index, 0, keepdims=False)
    mine_live = lax.dynamic_index_in_dim(live, group_index, 0, keepdims=False)
    mine_owner = lax.dynamic_index_in_dim(owners, group_index, 0, keepdims=False)
    mine_rows = lax.dynamic_index_in_dim(accept_rows, group_index, 0, keepdims=False)
    ranks = jnp.sum((jnp.cumsum(mine, axis=0) - mine) * mine, axis=1)
    local = jnp.where(mine_live, mine_owner * slots + ranks, -1)
    match = (local[None, :] == jnp.arange(group_count * slots, dtype=jnp.int32)[:, None]).astype(
        jnp.int32
    )
    send_index = jnp.sum(match * mine_rows[None, :], axis=1)
    send_live = jnp.sum(match, axis=1)
    per_pair = jnp.sum(onehot, axis=1)
    valid = (jnp.arange(slots, dtype=jnp.int32)[None, None, :] < per_pair.T[:, :, None]).astype(
        jnp.float32
    )
    return (send_index, send_live, valid.reshape(-1))


def row_backward(combined, target, gain, valid, total):
    squares = lax.psum(jnp.sum(combined * combined, axis=1), "group")
    scale = lax.rsqrt(squares / D + epsilon)
    normed = combined * scale[:, None] * gain[None, :]
    slope = valid[:, None] * (normed - target.astype(jnp.float32)) / total
    inner = lax.psum(jnp.sum(gain[None, :] * slope * combined, axis=1), "group")
    back = scale[:, None] * gain[None, :] * slope - combined * (scale**3 * inner / D)[:, None]
    return back.astype(jnp.bfloat16)


def shards(
    low_state,
    mid_state,
    residual,
    attention,
    o_weight,
    fc_weight,
    norm_gain,
    target,
    counts,
    accept_rows,
    owners,
):
    group_count = lax.axis_size("group")
    tensor_count = lax.axis_size("tensor")
    group_index = lax.axis_index("group")
    tensor_index = lax.axis_index("tensor")
    term = jnp.dot(attention, o_weight, preferred_element_type=jnp.float32)
    summed = lax.psum_scatter(
        term.astype(jnp.bfloat16), "tensor", scatter_dimension=1, tiled=True
    ).astype(jnp.float32)
    top_state = (residual.astype(jnp.float32) + summed).astype(jnp.bfloat16)
    send_index, send_live, valid = send_plan(
        counts, accept_rows, owners, group_count, group_index, SLOTS
    )
    states = jnp.concatenate([low_state, mid_state, top_state], axis=1)
    feature_count = states.shape[1]
    picked = jnp.take(states, send_index, axis=0) * send_live[:, None].astype(jnp.bfloat16)
    picked = picked.reshape(group_count, SLOTS, feature_count)
    received = lax.all_to_all(picked, "group", split_axis=0, concat_axis=0, tiled=True)
    gathered = lax.all_gather(
        received.reshape(group_count * SLOTS, feature_count), "group", axis=0, tiled=True
    )
    weights = fc_weight.reshape(feature_count, fc_weight.shape[2])
    total = jnp.sum(counts).astype(jnp.float32)
    train_rows = gathered.shape[0]
    share = train_rows // tensor_count
    block_rows = gathered
    combined = lax.psum_scatter(
        jnp.dot(block_rows, weights, preferred_element_type=jnp.float32).astype(jnp.bfloat16),
        "tensor",
        scatter_dimension=0,
        tiled=True,
    ).astype(jnp.float32)
    mine_valid = lax.dynamic_slice_in_dim(valid, tensor_index * share, share, 0)
    back = row_backward(combined, target, norm_gain, mine_valid, total)
    block_rows = gathered
    grad = lax.dot_general(
        block_rows,
        lax.all_gather(back, "tensor", axis=0, tiled=True),
        (((0,), (0,)), ((), ())),
        preferred_element_type=jnp.float32,
    )
    return (top_state, grad.reshape(fc_weight.shape))


def solution(mesh):
    in_specs = (
        P("group", "tensor"),
        P("group", "tensor"),
        P("group", "tensor"),
        P("group", "tensor"),
        P("tensor", None),
        P(None, "tensor", "group"),
        P("group"),
        P("tensor", "group"),
        P(),
        P(),
        P(),
    )
    out_specs = (P("group", "tensor"), P(None, "tensor", "group"))
    return jax.shard_map(shards, mesh=mesh, in_specs=in_specs, out_specs=out_specs, check_vma=False)
```

profile of v0, /device:TPU:1, one launch (start us, length us, event | category | flops | bytes accessed | tf_op | source)
XLA Modules:
  0.0 481.0 jit_solution(17391124530808323637)
XLA Ops:
  7.2 11.4 %convolution_convert_fusion = bf16[512,8192]{1,0:T(8,128)(2,1)} fusion(bf16[512,512]{1,0:T(8,128)(2,1)} %param.14, bf16[512,8192]{1,0:T(8,128)(2,1)} %param.15), kind=kOutput, calls=%fused_computation.1 | convolution fusion | flops 4299161600 | bytes 17301504 | tf_op jit(solution)/shard_map/dot_general | solution.py:65
  18.8 0.6 copy-done.5
  19.4 1.1 reduce-window.6
  20.9 0.7 dynamic-slice_select_fusion
  21.7 0.2 convert_reduce_fusion
  22.1 101.3 %reduce-scatter.3.cloned.1.call-done = bf16[512,512]{1,0:T(8,128)(2,1)} async-done(((bf16[512,8192]{1,0:T(8,128)(2,1)}), bf16[512,512]{1,0:T(8,128)(2,1)}) %reduce-scatter.3.cloned.1.call-update) | async-done | bytes 524304 | tf_op jit(solution)/shard_map/reduce_scatter | solution.py:66
  123.4 1.3 add_convert_fusion
  124.7 0.8 copy-done.1
  125.5 2.4 pad_maximum_fusion
  128.0 4.5 gather_fusion
  132.4 1.3 select_multiply_fusion
  133.7 14.9 %all_to_all.5 = bf16[8,32,1536]{2,1,0:T(8,128)(2,1)} all-to-all(bf16[8,32,1536]{2,1,0:T(8,128)(2,1)S(1)} %select_multiply_fusion), channel_id=1, replica_groups=mesh['group'=8,'tensor'=16] {'group'}, dimensions={0} | all-to-all | bytes 1572864 | tf_op jit(solution)/shard_map/all_to_all | solution.py:77
  148.8 128.5 %all-gather.3.cloned.1.call-done = bf16[2048,1536]{1,0:T(8,128)(2,1)} async-done(((bf16[256,1536]{1,0:T(8,128)(2,1)}), bf16[2048,1536]{1,0:T(8,128)(2,1)}) %all-gather.3.cloned.1.call-update) | async-done | bytes 6291472 | tf_op jit(solution)/shard_map/all_gather | solution.py:78
  277.3 11.0 %convolution_convert_fusion.1 = bf16[2048,1024]{1,0:T(8,128)(2,1)} fusion(bf16[2048,1536]{1,0:T(8,128)(2,1)} %all-gather.3.cloned.1.call-done, bf16[1536,1024]{1,0:T(8,128)(2,1)S(1)} %bitcast.27), kind=kOutput, calls=%fused_computation.2 | convolution fusion | flops 6444548096 | bytes 13631488 | tf_op jit(solution)/shard_map/dot_general | solution.py:87
  288.3 0.7 reduce_sum.77
  289.6 0.2 fusion.11
  290.1 78.1 %reduce-scatter.5.cloned.1.call-done = bf16[128,1024]{1,0:T(8,128)(2,1)} async-done(((bf16[2048,1024]{1,0:T(8,128)(2,1)}), bf16[128,1024]{1,0:T(8,128)(2,1)}) %reduce-scatter.5.cloned.1.call-update) | async-done | bytes 262160 | tf_op jit(solution)/shard_map/reduce_scatter | solution.py:86
  368.2 1.1 fusion
  369.3 15.5 %psum.14 = f32[128]{0:T(128)S(1)} all-reduce(f32[128]{0:T(128)S(1)} %fusion), channel_id=1, replica_groups=mesh['group'=8,'tensor'=16] {'group'}, use_global_device_ids=true, to_apply=%region_8.9 | all-reduce | flops 128 | bytes 1024 | tf_op jit(solution)/shard_map/psum | solution.py:39
  384.9 1.3 fusion.5
  386.2 12.7 %psum.15 = f32[128]{0:T(128)S(1)} all-reduce(f32[128]{0:T(128)S(1)} %fusion.5), channel_id=1, replica_groups=mesh['group'=8,'tensor'=16] {'group'}, use_global_device_ids=true, to_apply=%region_12.13 | all-reduce | flops 128 | bytes 1024 | tf_op jit(solution)/shard_map/psum | solution.py:43
  398.9 2.0 fusion.7
  400.9 61.8 %all-gather.5.cloned.1.call-done = bf16[2048,1024]{1,0:T(8,128)(2,1)} async-done(((bf16[128,1024]{1,0:T(8,128)(2,1)}), bf16[2048,1024]{1,0:T(8,128)(2,1)}) %all-gather.5.cloned.1.call-update) | async-done | bytes 4194320 | tf_op jit(solution)/shard_map/all_gather | solution.py:97
  462.7 11.8 %fusion.15 = f32[1536,1024]{1,0:T(8,128)} fusion(bf16[2048,1536]{1,0:T(8,128)(2,1)} %all-gather.3.cloned.1.call-done, bf16[2048,1024]{1,0:T(8,128)(2,1)} %all-gather.5.cloned.1.call-done), kind=kOutput, calls=%fused_computation.42 | convolution fusion | flops 6442450944 | bytes 16777216 | tf_op jit(solution)/shard_map/dot_general | solution.py:95
  (37 shorter events, 1.2 us)
Async XLA Ops:
  7.2 270.1 %copy-start = (bf16[3,512,1024]{2,1,0:T(8,128)(2,1)S(1)}, bf16[3,512,1024]{2,1,0:T(8,128)(2,1)}, u32[]{:S(2)}) copy-start(bf16[3,512,1024]{2,1,0:T(8,128)(2,1)} %param.16) | copy-start | bytes 9437188
  7.2 116.2 %reduce-scatter.3.cloned.1.call-start = ((), (), s32[]{:S(2)}) async-start(), calls=%async_computation.3 | async-start | bytes 8912896 | tf_op jit(solution)/shard_map/reduce_scatter | solution.py:66
  18.7 0.7 copy-start.5
  18.7 0.7 copy-start.3
  18.7 258.6 %all-gather.3.cloned.1.call-start = ((), (), s32[]{:S(2)}) async-start(), calls=%async_computation.4 | async-start | bytes 7077888 | tf_op jit(solution)/shard_map/all_gather | solution.py:78
  124.7 0.8 copy-start.1
  148.7 219.5 %reduce-scatter.5.cloned.1.call-start = ((), (), s32[]{:S(2)}) async-start(), calls=%async_computation.5 | async-start | bytes 4456448 | tf_op jit(solution)/shard_map/reduce_scatter | solution.py:86
  288.3 96.6 %copy-start.2 = (bf16[128,1024]{1,0:T(8,128)(2,1)S(1)}, bf16[128,1024]{1,0:T(8,128)(2,1)}, u32[]{:S(2)}) copy-start(bf16[128,1024]{1,0:T(8,128)(2,1)} %param.18) | copy-start | bytes 786436
  288.3 96.6 %copy-start.4 = (f32[1024]{0:T(1024)S(1)}, f32[1024]{0:T(1024)}, u32[]{:S(2)}) copy-start(f32[1024]{0:T(1024)} %param.17) | copy-start | bytes 12292
  288.3 174.4 %all-gather.5.cloned.1.call-start = ((), (), s32[]{:S(2)}) async-start(), calls=%async_computation.6 | async-start | bytes 4456448 | tf_op jit(solution)/shard_map/all_gather | solution.py:97
Sparse Core Ops, SparseCore 0:
  18.8 104.5 reduce-scatter.2
  148.8 128.3 all-gather.2
  288.4 79.7 reduce-scatter.4
  401.1 61.5 all-gather.4
where the time goes:
time: 482 us; the launch traced here: 481 us
  waiting for transfers between devices  370 us (77%)
  blocking collectives  43.2 us (9%)
  matrix products  34.2 us (7%)
  between operations  14.5 us (3%)
  other arithmetic  12.8 us (3%)
  local copies, waits for them, and re-layouts  6.48 us (1%)
    all_gather x1, waiting for transfers between devices, shards(): lax.all_gather(received.reshape(group_count * SLOTS, feature_count), 'gro...  128 us
    reduce_scatter x1, waiting for transfers between devices, shards(): lax.psum_scatter(term.astype(jnp.bfloat16), 'tensor', scatter_dimension=1...  101 us
    reduce_scatter x1, waiting for transfers between devices, shards(): lax.psum_scatter(jnp.dot(block_rows, weights, preferred_element_type=jnp....  78.1 us
    all_gather x1, waiting for transfers between devices, shards(): lax.all_gather(back, 'tensor', axis=0, tiled=True)  61.8 us
    psum x1, blocking collectives, row_backward(): squares = lax.psum(jnp.sum(combined * combined, axis=1), 'group')  15.5 us
    all_to_all x1, blocking collectives, shards(): lax.all_to_all(picked, 'group', split_axis=0, concat_axis=0, tiled=True)  14.9 us
    psum x1, blocking collectives, row_backward(): inner = lax.psum(jnp.sum(gain[None, :] * slope * combined, axis=1), 'group')  12.7 us
    dot_general x1, matrix products, shards(): lax.dot_general(block_rows, lax.all_gather(back, 'tensor', axis=0, tiled=...  11.8 us
  transfers between devices with their start and end apart: 4, of which 4 were waited for; matrix products, arithmetic and copies ran while one was open for 1% of the time, Pallas kernels for 0%

commit v1 on v0

v1 whole, which is shorter than its diff:
```python
import functools

import jax
import jax.numpy as jnp
from jax import lax
from jax.experimental import pallas as pl
from jax.experimental.pallas import tpu as pltpu
from jax.sharding import PartitionSpec as P

D = 8192
SLOTS = 32
MESH = pl.DeviceIdType.MESH

epsilon = 1e-05


def row_plan(counts, accept_rows, owners, group_count, group_index, slots):
    rows = owners.shape[1]
    count = lax.dynamic_index_in_dim(counts, group_index, 0, keepdims=False)
    owner = lax.dynamic_index_in_dim(owners, group_index, 0, keepdims=False)
    accept = lax.dynamic_index_in_dim(accept_rows, group_index, 0, keepdims=False)
    index = jnp.arange(rows, dtype=jnp.int32)
    live = index < count
    earlier = (owner[None, :] == owner[:, None]) & (index[None, :] < index[:, None]) & live[None, :]
    ranks = jnp.sum(earlier.astype(jnp.int32), axis=1)
    place = jnp.where(live, owner * slots + ranks, -1)
    match = place[None, :] == index[:, None]
    taken = jnp.sum(match.astype(jnp.int32), axis=1)
    chosen = jnp.sum(jnp.where(match, index[None, :], 0), axis=1)
    free = jnp.sum(jnp.where(index[None, :] < index[:, None], 1 - taken[None, :], 0), axis=1)
    chosen = jnp.where(taken > 0, chosen, count + free)
    return jnp.sum(jnp.where(chosen[:, None] == index[None, :], accept[None, :], 0), axis=1)


def place_in_mesh():
    group, tensor = lax.axis_index("group"), lax.axis_index("tensor")
    return group // 2, group % 2, tensor // 4, (tensor // 2) % 2, tensor % 2


def device(z, low, y, high, core):
    return (z * 2 + low, y * 4 + high * 2 + core)


def enter(peers):
    barrier = pltpu.get_barrier_semaphore()
    for peer in peers:
        pl.semaphore_signal(barrier, inc=1, device_id=peer, device_id_type=MESH)
    pl.semaphore_wait(barrier, len(peers))


def send(src, dst, send_sem, recv_sem, peer):
    return pltpu.make_async_remote_copy(
        src_ref=src, dst_ref=dst, send_sem=send_sem, recv_sem=recv_sem,
        device_id=peer, device_id_type=MESH,
    )


class RingGather:
    def __init__(self, block, ring, pair, other, up, down, sends, recvs):
        self.block, self.ring, self.pair = block, ring, pair
        self.other, self.up, self.down = other, up, down
        self.sends, self.recvs = sends, recvs
        self.started = []

    def _go(self, src, dst, k, peer):
        copy = send(src, dst, self.sends.at[k], self.recvs.at[k], peer)
        copy.start()
        self.started.append(copy)

    def _arrived(self, ref, k, peer):
        send(ref, ref, self.sends.at[k], self.recvs.at[k], peer).wait_recv()

    def own(self, src):
        mine = self.block(self.ring, self.pair, None)
        self._go(src, mine, 1, self.up)
        self._go(src, mine, 2, self.down)
        self._go(src, mine, 0, self.other)

    def relay_pair(self):
        ref = self.block(self.ring, 1 - self.pair, None)
        self._arrived(ref, 0, self.other)
        self._go(ref, ref, 3, self.up)
        self._go(ref, ref, 4, self.down)
        return [ref]

    def relay_ring(self, flip):
        side = 1 - self.pair if flip else self.pair
        below, above = (self.ring + 3) % 4, (self.ring + 1) % 4
        k = 2 if flip else 0
        low, high = self.block(below, side, None), self.block(above, side, None)
        self._arrived(low, 1 + k, self.down)
        half = self.block(below, side, 0)
        self._go(half, half, 5 + k, self.up)
        self._arrived(high, 2 + k, self.up)
        half = self.block(above, side, 1)
        self._go(half, half, 6 + k, self.down)
        return [low, high]

    def last(self, flip):
        side = 1 - self.pair if flip else self.pair
        far = (self.ring + 2) % 4
        k = 2 if flip else 0
        first, second = self.block(far, side, 0), self.block(far, side, 1)
        self._arrived(first, 5 + k, self.down)
        self._arrived(second, 6 + k, self.up)
        return [first, second]

    def drain(self):
        for copy in self.started:
            copy.wait_send()


class ChipScatter:
    def __init__(self, acc, first, second, y, high, peers, partner, bufs, sends, recvs):
        self.acc, self.first, self.second = acc, first, second
        self.y, self.high, self.peers, self.partner = y, high, peers, partner
        self.ya, self.xb, self.xs, self.xa, self.bs, self.yb, self.own = bufs
        self.sends, self.recvs = sends, recvs
        self.copies = {}

    def _go(self, src, dst, k, peer):
        copy = send(src, dst, self.sends.at[k], self.recvs.at[k], peer)
        copy.start()
        self.copies[k] = copy

    def start(self):
        for d in (1, 2, 3):
            to = (self.y + d) % 4
            self._go(self.acc.at[to, :, self.first], self.ya.at[d - 1], d - 1, self.peers[d - 1])
        self._go(self.acc.at[:, 1 - self.high, self.second], self.xb, 3, self.partner)

    def middle(self):
        for d in (1, 2, 3):
            self.copies[d - 1].wait_recv()

        def along_y(side):
            total = self.acc[self.y, side, self.first].astype(jnp.float32)
            for d in (0, 1, 2):
                total += self.ya[d, side].astype(jnp.float32)
            return total

        self.xs[...] = along_y(1 - self.high).astype(jnp.bfloat16)
        self._go(self.xs, self.xa, 4, self.partner)
        self.own[0] = along_y(self.high)
        self.copies[3].wait_recv()
        for d in (1, 2, 3):
            to = (self.y + d) % 4
            pair = self.acc[to, self.high, self.second].astype(jnp.float32) + self.xb[to].astype(jnp.float32)
            self.bs[d - 1] = pair.astype(jnp.bfloat16)
            self._go(self.bs.at[d - 1], self.yb.at[d - 1], 4 + d, self.peers[d - 1])
        self.own[1] = self.acc[self.y, self.high, self.second].astype(jnp.float32) + self.xb[self.y].astype(jnp.float32)

    def finish(self):
        self.copies[4].wait_recv()
        first = self.own[0] + self.xa[...].astype(jnp.float32)
        total = self.own[1]
        for d in (1, 2, 3):
            self.copies[4 + d].wait_recv()
            total += self.yb[d - 1].astype(jnp.float32)
        return first, total

    def drain(self):
        for copy in self.copies.values():
            copy.wait_send()


def scatter_buffers(rows, columns):
    return [
        pltpu.VMEM((3, 2, rows, columns), jnp.bfloat16),
        pltpu.VMEM((4, rows, columns), jnp.bfloat16),
        pltpu.VMEM((rows, columns), jnp.bfloat16),
        pltpu.VMEM((rows, columns), jnp.bfloat16),
        pltpu.VMEM((3, rows, columns), jnp.bfloat16),
        pltpu.VMEM((3, rows, columns), jnp.bfloat16),
        pltpu.VMEM((2, rows, columns), jnp.float32),
        pltpu.SemaphoreType.DMA((8,)),
        pltpu.SemaphoreType.DMA((8,)),
    ]


def join_kernel(
    rowp_ref, low_ref, mid_ref, res_ref, att_ref, w_ref,
    top_ref, gath_ref,
    wbuf, psend, prec, acc, lmbuf, topbuf, attp, resp,
    a0, a1, a2, a3, a4, a5, a6, as_, ar_,
    b0, b1, b2, b3, b4, b5, b6, bs_, br_,
    wsem, psem, qsem, gsend, grecv, hsend, hrecv, lsem,
):
    z, xl, y, xh, c = place_in_mesh()
    g = z * 2 + xl
    n_rows = att_ref.shape[0]
    half = n_rows // 2
    width = att_ref.shape[1]
    quarter = half // 2
    loads = [
        pltpu.make_async_copy(w_ref.at[:, pl.ds(k * width, width)], wbuf.at[k], wsem.at[k]) for k in range(16)
    ]
    for load in loads:
        load.start()
    sib = device(z, xl, y, xh, 1 - c)
    partner = device(z, xl, y, 1 - xh, c)
    peers = [device(z, xl, (y + d) % 4, xh, c) for d in (1, 2, 3)]
    other = device(z, 1 - xl, y, xh, c)
    up, down = device((z + 1) % 4, xl, y, xh, c), device((z + 3) % 4, xl, y, xh, c)
    enter([sib, partner, *peers, other, up, down])

    def gather(first, size, sends, recvs):
        def block(r, s, part):
            owners = pl.ds(0, 8) if part is None else pl.ds(part * 4, 4)
            return gath_ref.at[owners, r * 2 + s, :, pl.ds(first, size)]
        return RingGather(block, z, xl, other, up, down, sends, recvs)

    pick = (rowp_ref[...] == lax.broadcasted_iota(jnp.int32, (n_rows, n_rows), 1)).astype(jnp.bfloat16)

    def picked(ref, rows):
        return jnp.dot(pick[:rows], ref[...], preferred_element_type=jnp.float32)

    lmbuf[:, :, :width] = picked(low_ref, half).astype(jnp.bfloat16).reshape(8, half // 8, width)
    lmbuf[:, :, width:] = picked(mid_ref, half).astype(jnp.bfloat16).reshape(8, half // 8, width)
    lm = gather(0, 2 * width, gsend, grecv)
    lm.own(lmbuf)
    keep_lm = pltpu.make_async_copy(lmbuf, gath_ref.at[:, g, :, pl.ds(0, 2 * width)], lsem.at[0])
    keep_lm.start()
    attp[...] = picked(att_ref, n_rows).astype(jnp.bfloat16)
    for load in loads:
        load.wait()

    def to_sibling(r, b):
        rows = pl.ds(r * half, half)
        return send(psend.at[b, rows], prec.at[b, rows], psem.at[r, b], qsem.at[r, b], sib)

    def product(r):
        rows = pl.ds(r * half, half)

        def theirs(b, _):
            part = jnp.dot(attp[rows], wbuf[2 * b + 1 - c], preferred_element_type=jnp.float32)
            psend[b, rows] = part.astype(jnp.bfloat16)
            to_sibling(r, b).start()
            return 0

        lax.fori_loop(0, 8, theirs, 0)

        def ours(b, _):
            part = jnp.dot(attp[rows], wbuf[2 * b + c], preferred_element_type=jnp.float32)
            to_sibling(r, b).wait_recv()
            acc[b // 2, b % 2, rows] = (part + prec[b, rows].astype(jnp.float32)).astype(jnp.bfloat16)
            return 0

        lax.fori_loop(0, 8, ours, 0)

    def scatter(r, bufs, sends, recvs):
        return ChipScatter(
            acc, pl.ds(r * half, quarter), pl.ds(r * half + quarter, quarter), y, xh, peers, partner, bufs, sends, recvs
        )

    product(0)
    rs0 = scatter(0, (a0, a1, a2, a3, a4, a5, a6), as_, ar_)
    rs0.start()
    lm.relay_pair()
    product(1)
    resp[...] = picked(res_ref, n_rows)
    rs0.middle()
    lm.relay_ring(False)
    first, second = rs0.finish()
    first = (resp[:quarter] + first).astype(jnp.bfloat16)
    second = (resp[quarter:half] + second).astype(jnp.bfloat16)
    topbuf[:4] = first.reshape(4, half // 8, width)
    topbuf[4:] = second.reshape(4, half // 8, width)
    top = gather(2 * width, width, hsend, hrecv)
    top.own(topbuf)
    keep_top = pltpu.make_async_copy(topbuf, gath_ref.at[:, g, :, pl.ds(2 * width, width)], lsem.at[1])
    keep_top.start()
    rs1 = scatter(1, (b0, b1, b2, b3, b4, b5, b6), bs_, br_)
    rs1.start()
    top_ref[:quarter] = first
    top_ref[quarter:half] = second
    lm.relay_ring(True)
    top.relay_pair()
    rs1.middle()
    top.relay_ring(False)
    top.relay_ring(True)
    first, second = rs1.finish()
    top_ref[half:half + quarter] = (resp[half:half + quarter] + first).astype(jnp.bfloat16)
    top_ref[half + quarter:] = (resp[half + quarter:] + second).astype(jnp.bfloat16)
    for flip in (False, True):
        lm.last(flip)
        top.last(flip)

    def sent(b, _):
        to_sibling(0, b).wait_send()
        to_sibling(1, b).wait_send()
        return 0

    lax.fori_loop(0, 8, sent, 0)
    for part in (lm, top, rs0, rs1):
        part.drain()
    keep_lm.wait()
    keep_top.wait()


def back_kernel(
    x_ref, w_ref, target_ref, gain_ref, weight_ref,
    back_ref,
    psend, prec, acc, stat, stats, own_back,
    a0, a1, a2, a3, a4, a5, a6, as_, ar_,
    psem, qsem, ssend, srecv, gsend, grecv, dsend, drecv, lsem,
):
    z, xl, y, xh, c = place_in_mesh()
    g = z * 2 + xl
    tensor = lax.axis_index("tensor")
    sib = device(z, xl, y, xh, 1 - c)
    partner = device(z, xl, y, 1 - xh, c)
    peers = [device(z, xl, (y + d) % 4, xh, c) for d in (1, 2, 3)]
    replicas = [((g + d) % 8, tensor) for d in range(1, 8)]
    enter([sib, partner, *peers, *replicas])
    features = x_ref.shape[3]
    columns = w_ref.shape[1]
    share = target_ref.shape[0]
    step = columns // 4

    def to_sibling(n):
        return send(psend.at[n], prec.at[n], psem.at[n], qsem.at[n], sib)

    def part(core, n):
        rows = x_ref[:, pl.ds(core * 4, 4)].reshape(8 * share, features)
        return jnp.dot(rows, w_ref[:, pl.ds(pl.multiple_of(n * step, step), step)], preferred_element_type=jnp.float32)

    def theirs(n, _):
        psend[n] = part(1 - c, n).astype(jnp.bfloat16)
        to_sibling(n).start()
        return 0

    lax.fori_loop(0, 4, theirs, 0)

    def ours(n, _):
        mine = part(c, n)
        to_sibling(n).wait_recv()
        both = (mine + prec[n].astype(jnp.float32)).astype(jnp.bfloat16)
        acc[:, :, :, pl.ds(pl.multiple_of(n * step, step), step)] = both.reshape(4, 2, share, step)
        return 0

    lax.fori_loop(0, 4, ours, 0)
    rs = ChipScatter(
        acc, pl.ds(0, share // 2), pl.ds(share // 2, share // 2), y, xh, peers, partner,
        (a0, a1, a2, a3, a4, a5, a6), as_, ar_,
    )
    rs.start()
    rs.middle()
    first, second = rs.finish()
    combined = jnp.concatenate([first, second], axis=0)
    gain = gain_ref[...]
    target = target_ref[...].astype(jnp.float32)
    gained = combined * gain
    lane = lax.broadcasted_iota(jnp.int32, (share, 128), 1)
    sums = jnp.where(
        lane == 0, jnp.sum(combined * combined, axis=1, keepdims=True),
        jnp.where(
            lane == 1, jnp.sum(gained * gained, axis=1, keepdims=True),
            jnp.sum(gained * target, axis=1, keepdims=True),
        ),
    )
    stat[...] = sums.T[:8]
    copies = [
        send(stat, stats.at[d - 1], ssend.at[d - 1], srecv.at[d - 1], replicas[d - 1]) for d in range(1, 8)
    ]
    for copy in copies:
        copy.start()
    total = stat[...]
    for d in range(7):
        copies[d].wait_recv()
        total += stats[d]
    total = jnp.concatenate([total, jnp.zeros((120, share), jnp.float32)], axis=0).T
    scale = lax.rsqrt(total[:, 0:1] / D + epsilon)
    weight = weight_ref[...]
    inner = weight * (scale * total[:, 1:2] - total[:, 2:3])
    slope = weight * (gained * scale - target)
    back = scale * gain * slope - combined * (scale * scale * scale * inner / D)
    own_back[...] = back.astype(jnp.bfloat16)

    def block(r, s, half):
        if half is None:
            return back_ref.at[r * 2 + s, c]
        return back_ref.at[r * 2 + s, c, pl.ds(half * (share // 2), share // 2)]

    ag = RingGather(block, y, xh, partner, peers[0], peers[2], gsend, grecv)
    ag.own(own_back)
    keep = pltpu.make_async_copy(own_back, back_ref.at[y * 2 + xh, c], lsem.at[0])
    keep.start()
    over = []

    def across(k, src, ref):
        copy = send(src, ref, dsend.at[k], drecv.at[k], sib)
        copy.start()
        over.append(copy)

    across(0, own_back, block(y, xh, None))
    across(1, *ag.relay_pair() * 2)
    k = 2
    for flip in (False, True):
        for ref in ag.relay_ring(flip):
            across(k, ref, ref)
            k += 1
    for flip in (False, True):
        for ref in ag.last(flip):
            across(k, ref, ref)
            k += 1

    def theirs_at(r, s, half):
        if half is None:
            return back_ref.at[r * 2 + s, 1 - c]
        return back_ref.at[r * 2 + s, 1 - c, pl.ds(half * (share // 2), share // 2)]

    below, above, far = (y + 3) % 4, (y + 1) % 4, (y + 2) % 4
    landed = [
        (y, xh, None), (y, 1 - xh, None),
        (below, xh, None), (above, xh, None), (below, 1 - xh, None), (above, 1 - xh, None),
        (far, xh, 0), (far, xh, 1), (far, 1 - xh, 0), (far, 1 - xh, 1),
    ]
    for k, at in enumerate(landed):
        ref = theirs_at(*at)
        send(ref, ref, dsend.at[k], drecv.at[k], sib).wait_recv()
    for copy in (*copies, *over):
        copy.wait_send()

    def sent(n, _):
        to_sibling(n).wait_send()
        return 0

    lax.fori_loop(0, 4, sent, 0)
    rs.drain()
    ag.drain()
    keep.wait()


def shards(
    low_state, mid_state, residual, attention, o_weight, fc_weight, norm_gain, target, counts, accept_rows, owners,
):
    group_count = lax.axis_size("group")
    group_index = lax.axis_index("group")
    tensor_index = lax.axis_index("tensor")
    rows, width = attention.shape
    half, quarter = rows // 2, rows // 4
    slots = half // group_count
    rowp = row_plan(counts, accept_rows, owners, group_count, group_index, slots)
    vmem = pl.BlockSpec(memory_space=pltpu.VMEM)
    anywhere = pl.BlockSpec(memory_space=pl.ANY)
    dma = pltpu.SemaphoreType.DMA
    bf16 = jnp.bfloat16
    top_perm, gathered = pl.pallas_call(
        join_kernel,
        out_shape=(
            jax.ShapeDtypeStruct((rows, width), bf16),
            jax.ShapeDtypeStruct((8, 8, slots, 3 * width), bf16),
        ),
        in_specs=[vmem, vmem, vmem, vmem, vmem, anywhere],
        out_specs=(vmem, anywhere),
        scratch_shapes=[
            pltpu.VMEM((16, width, width), bf16),
            pltpu.VMEM((8, rows, width), bf16),
            pltpu.VMEM((8, rows, width), bf16),
            pltpu.VMEM((4, 2, rows, width), bf16),
            pltpu.VMEM((8, slots, 2 * width), bf16),
            pltpu.VMEM((8, slots, width), bf16),
            pltpu.VMEM((rows, width), bf16),
            pltpu.VMEM((rows, width), jnp.float32),
            *scatter_buffers(quarter, width),
            *scatter_buffers(quarter, width),
            dma((16,)), dma((2, 8)), dma((2, 8)), dma((9,)), dma((9,)), dma((9,)), dma((9,)), dma((2,)),
        ],
        compiler_params=pltpu.CompilerParams(collective_id=0, has_side_effects=True, vmem_limit_bytes=48 << 20),
        cost_estimate=pl.CostEstimate(flops=2 * rows * width * D, bytes_accessed=16 << 20, transcendentals=0),
    )(rowp[:, None], low_state, mid_state, residual, attention, o_weight)

    share, columns = target.shape
    owner = tensor_index // 2
    first = (tensor_index % 2) * 4
    mine_owners = lax.dynamic_slice_in_dim(owners, first, 4, 0)
    mine_counts = lax.dynamic_slice_in_dim(counts, first, 4, 0)
    pairs = jnp.sum(
        ((mine_owners == owner) & (jnp.arange(rows, dtype=jnp.int32)[None, :] < mine_counts[:, None])).astype(jnp.int32),
        axis=1,
    )
    valid = (jnp.arange(slots, dtype=jnp.int32)[None, :] < pairs[:, None]).astype(jnp.float32)
    weight = valid.reshape(share, 1) / jnp.sum(counts).astype(jnp.float32)
    weights = fc_weight.reshape(3 * width, columns)
    back = pl.pallas_call(
        back_kernel,
        out_shape=jax.ShapeDtypeStruct((8, 2, share, columns), bf16),
        in_specs=[vmem] * 5,
        out_specs=anywhere,
        scratch_shapes=[
            pltpu.VMEM((4, 8 * share, columns // 4), bf16),
            pltpu.VMEM((4, 8 * share, columns // 4), bf16),
            pltpu.VMEM((4, 2, share, columns), bf16),
            pltpu.VMEM((8, share), jnp.float32),
            pltpu.VMEM((7, 8, share), jnp.float32),
            pltpu.VMEM((share, columns), bf16),
            *scatter_buffers(share // 2, columns),
            dma((4,)), dma((4,)), dma((7,)), dma((7,)), dma((9,)), dma((9,)), dma((10,)), dma((10,)), dma((1,)),
        ],
        compiler_params=pltpu.CompilerParams(collective_id=1, has_side_effects=True, vmem_limit_bytes=48 << 20),
        cost_estimate=pl.CostEstimate(flops=4 * rows * 12 * width * columns, bytes_accessed=16 << 20, transcendentals=0),
    )(gathered, weights, target, norm_gain[None, :], weight)
    grad = lax.dot_general(
        gathered.reshape(16 * share, 3 * width),
        back.reshape(16 * share, columns),
        (((0,), (0,)), ((), ())),
        preferred_element_type=jnp.float32,
    )
    put = (rowp[:, None] == jnp.arange(rows, dtype=jnp.int32)[None, :]).astype(bf16)
    top_state = lax.dot_general(
        put, top_perm, (((0,), (0,)), ((), ())), preferred_element_type=jnp.float32
    ).astype(bf16)
    return (top_state, grad.reshape(fc_weight.shape))


def solution(mesh):
    in_specs = (
        P("group", "tensor"),
        P("group", "tensor"),
        P("group", "tensor"),
        P("group", "tensor"),
        P("tensor", None),
        P(None, "tensor", "group"),
        P("group"),
        P("tensor", "group"),
        P(),
        P(),
        P(),
    )
    out_specs = (P("group", "tensor"), P(None, "tensor", "group"))
    return jax.shard_map(shards, mesh=mesh, in_specs=in_specs, out_specs=out_specs, check_vma=False)
```

time: 482 us -> 163 us (0.34)
  waiting for transfers between devices: 370 us -> 0 us
  Pallas kernels: 0 us -> 127 us
  blocking collectives: 43.2 us -> 0 us
  matrix products: 34.2 us -> 13 us
  between operations: 14.5 us -> 1.42 us
  local copies, waits for them, and re-layouts: 6.48 us -> 15.8 us
  other arithmetic: 12.8 us -> 5.26 us
    all_gather x2 -> x0, waiting for transfers between devices: 190 us -> none  [the longest x1 128 us: shards(): lax.all_gather(received.reshape(group_count * SLOTS, feature_count), 'gro...]
    reduce_scatter x2 -> x0, waiting for transfers between devices: 179 us -> none  [the longest x1 101 us: shards(): lax.psum_scatter(term.astype(jnp.bfloat16), 'tensor', scatter_dimension=1...]
    pallas_call x0 -> x2, Pallas kernels: none -> 127 us  [the longest x1 65.9 us: shards(): pl.pallas_call(back_kernel, out_shape=jax.ShapeDtypeStruct((8, 2, share,...]
    psum x2 -> x0, blocking collectives: 28.3 us -> none  [the longest x1 15.5 us: row_backward(): squares = lax.psum(jnp.sum(combined * combined, axis=1), 'group')]
    dot_general x3 -> x2, matrix products: 34.2 us -> 13 us  [the longest x1 11.6 us: shards(): lax.dot_general(gathered.reshape(16 * share, 3 * width), back.reshape(16...]
    all_to_all x1 -> x0, blocking collectives: 14.9 us -> none  [shards(): lax.all_to_all(picked, 'group', split_axis=0, concat_axis=0, tiled=True)]
    dot_general x0 -> x1, local copies, waits for them, and re-layouts: none -> 8.67 us  [shards(): lax.dot_general(gathered.reshape(16 * share, 3 * width), back.reshape(16...]
  transfers between devices with their start and end apart: 4 -> 0, of which waited for: 4 -> 0; matrix products, arithmetic and copies ran while one was open for 1% -> 0% of each run, Pallas kernels for 0% -> 0%
where the time goes in v1:
time: 163 us
  Pallas kernels  127 us (78%)
  local copies, waits for them, and re-layouts  15.8 us (10%)
  matrix products  13 us (8%)
  other arithmetic  5.26 us (3%)
    pallas_call x1, Pallas kernels, shards(): pl.pallas_call(back_kernel, out_shape=jax.ShapeDtypeStruct((8, 2, share,...  65.9 us
    pallas_call x1, Pallas kernels, shards(): pl.pallas_call(join_kernel, out_shape=(jax.ShapeDtypeStruct((rows, width)...  61.4 us
    dot_general x1, matrix products, shards(): lax.dot_general(gathered.reshape(16 * share, 3 * width), back.reshape(16...  11.6 us
    dot_general x1, local copies, waits for them, and re-layouts, shards(): lax.dot_general(gathered.reshape(16 * share, 3 * width), back.reshape(16...  8.67 us
    unnamed x14, local copies, waits for them, and re-layouts  4.17 us

profile of v1, /device:TPU:1, one launch (start us, length us, event | category | flops | bytes accessed | tf_op | source)
XLA Modules:
  0.0 162.8 jit_solution(415071886148778568)
XLA Ops:
  0.7 1.2 dynamic_slice.17
  1.9 1.3 reduce_sum.72
  3.9 0.7 iota_compare_fusion.7
  4.5 0.7 dynamic_slice.21
  5.3 0.9 convert_reduce_fusion.2
  6.2 0.1 fusion.4
  6.2 0.7 constant_dynamic-slice_fusion
  7.0 0.3 convert_reduce_fusion.1
  7.3 0.7 compare_select_fusion
  7.9 0.4 convert_reduce_fusion
  8.3 0.1 select_reduce_fusion.1
  8.4 0.7 add_select_fusion
  9.1 0.2 select_reduce_fusion
  9.4 0.1 div.22.weight_ref
  9.5 0.1 copy.18.rowp_ref
  9.6 1.0 copy-done.1
  10.7 1.0 copy-done.2
  11.7 1.0 copy-done.3
  12.8 1.0 copy-done.4
  13.8 61.4 %shard_map.122 = (bf16[512,512]{1,0:T(8,128)(2,1)S(1)}, bf16[8,8,32,1536]{3,2,1,0:T(8,128)(2,1)}) custom-call(s32[512,1]{1,0:T(8,128)S(1)} %copy.18.rowp_ref, bf16[512,512]{1,0:T(8,128)(2,1)S(1)} %copy-done.1, bf16[512,512]{1,0:T(8,128)(2,1)S(1)} %copy-done.2, bf16[512,512]{1,0:T(8,128)(2,1)S(1)} %copy-done.3, bf16[512,512]{1,0:T(8,128)(2,1)S(1)} %copy-done.4, ...), custom_call_target="tpu_custom_call" | custom-call | flops 4294967296 | bytes 16777216 | tf_op jit(solution)/shard_map/pallas_call | solution.py:449
  75.2 1.4 convolution_convert_fusion
  76.6 65.9 %shard_map.123 = bf16[8,2,128,1024]{3,2,1,0:T(8,128)(2,1)} custom-call(bf16[8,8,32,1536]{3,2,1,0:T(8,128)(2,1)} %get-tuple-element.5.x_ref, bf16[1536,1024]{1,0:T(8,128)(2,1)S(1)} %bitcast.18, bf16[128,1024]{1,0:T(8,128)(2,1)S(1)} %copy-done.5, f32[1,1024]{1,0:T(1,128)S(1)} %bitcast.19, f32[128,1]{1,0:T(8,128)S(1)} %div.22.weight_ref), custom_call_target="tpu_custom_call" | custom-call | flops 12884901888 | bytes 16777216 | tf_op jit(solution)/shard_map/pallas_call | solution.py:486
  142.5 8.7 %copy.19 = bf16[1536,2048]{1,0:T(8,128)(2,1)} copy(bf16[1536,2048]{0,1:T(8,128)(2,1)} %bitcast.20) | data formatting | bytes 12582912 | tf_op jit(solution)/shard_map/dot_general | solution.py:504
  151.2 11.6 %fusion.5 = f32[3,512,1024]{2,1,0:T(8,128)} fusion(bf16[3,512,2048]{2,1,0:T(8,128)(2,1)} %bitcast.21, bf16[2048,1024,1]{1,0,2:T(8,128)(2,1)} %bitcast.27), kind=kOutput, calls=%fused_computation.25 | convolution fusion | flops 6442450944 | bytes 16777216 | tf_op jit(solution)/shard_map/dot_general | solution.py:504
  (11 shorter events, 0.0 us)
Async XLA Ops:
  9.6 1.0 copy-start.1
  10.7 1.0 copy-start.2
  11.7 1.0 copy-start.3
  12.8 1.0 copy-start.4
  13.8 62.8 %copy-start = (bf16[3,512,1024]{2,1,0:T(8,128)(2,1)S(1)}, bf16[3,512,1024]{2,1,0:T(8,128)(2,1)}, u32[]{:S(2)}) copy-start(bf16[3,512,1024]{2,1,0:T(8,128)(2,1)} %param.16) | copy-start | bytes 9437188
  13.8 62.8 %copy-start.5 = (bf16[128,1024]{1,0:T(8,128)(2,1)S(1)}, bf16[128,1024]{1,0:T(8,128)(2,1)}, u32[]{:S(2)}) copy-start(bf16[128,1024]{1,0:T(8,128)(2,1)} %target_ref.1) | copy-start | bytes 786436
  13.8 62.8 %copy-start.6 = (f32[1024]{0:T(1024)S(1)}, f32[1024]{0:T(1024)}, u32[]{:S(2)}) copy-start(f32[1024]{0:T(1024)} %param.17) | copy-start | bytes 12292

commit v2 on v1

v2 whole, which is shorter than its diff:
```python
import jax
import jax.numpy as jnp
from jax import lax
from jax.experimental import pallas as pl
from jax.experimental.pallas import tpu as pltpu
from jax.sharding import PartitionSpec as P

D = 8192
SLOTS = 32
MESH = pl.DeviceIdType.MESH

epsilon = 1e-05


def place_in_mesh():
    group, tensor = lax.axis_index("group"), lax.axis_index("tensor")
    return group // 2, group % 2, tensor // 4, (tensor // 2) % 2, tensor % 2


def device(z, low, y, high, core):
    return (z * 2 + low, y * 4 + high * 2 + core)


def enter(peers):
    barrier = pltpu.get_barrier_semaphore()
    for peer in peers:
        pl.semaphore_signal(barrier, inc=1, device_id=peer, device_id_type=MESH)
    pl.semaphore_wait(barrier, len(peers))


def send(src, dst, send_sem, recv_sem, peer):
    return pltpu.make_async_remote_copy(
        src_ref=src, dst_ref=dst, send_sem=send_sem, recv_sem=recv_sem,
        device_id=peer, device_id_type=MESH,
    )


class RingGather:
    def __init__(self, block, other, up, down, sends, recvs):
        self.block, self.other, self.up, self.down = block, other, up, down
        self.sends, self.recvs = sends, recvs
        self.started = []

    def _go(self, at, k, peer, view):
        copy = send(self.block(*at, (0, 0)), self.block(*at, view), self.sends.at[k], self.recvs.at[k], peer)
        copy.start()
        self.started.append(copy)

    def _arrived(self, at, k, peer):
        ref = self.block(*at, (0, 0))
        send(ref, ref, self.sends.at[k], self.recvs.at[k], peer).wait_recv()
        return ref

    def own(self):
        self._go((0, 0, None), 1, self.up, (1, 0))
        self._go((0, 0, None), 2, self.down, (3, 0))
        self._go((0, 0, None), 0, self.other, (0, 1))

    def relay_pair(self):
        ref = self._arrived((0, 1, None), 0, self.other)
        self._go((0, 1, None), 3, self.up, (1, 0))
        self._go((0, 1, None), 4, self.down, (3, 0))
        return [ref]

    def relay_ring(self, flip):
        k = 2 * flip
        low = self._arrived((3, flip, None), 1 + k, self.down)
        self._go((3, flip, 0), 5 + k, self.up, (1, 0))
        high = self._arrived((1, flip, None), 2 + k, self.up)
        self._go((1, flip, 1), 6 + k, self.down, (3, 0))
        return [low, high]

    def last(self, flip):
        k = 2 * flip
        first = self._arrived((2, flip, 0), 5 + k, self.down)
        second = self._arrived((2, flip, 1), 6 + k, self.up)
        return [first, second]

    def drain(self):
        for copy in self.started:
            copy.wait_send()


class ChipScatter:
    def __init__(self, acc, first, second, y, high, peers, partner, bufs, sends, recvs):
        self.acc, self.first, self.second = acc, first, second
        self.y, self.high, self.peers, self.partner = y, high, peers, partner
        self.ya, self.xb, self.xs, self.xa, self.bs, self.yb, self.own = bufs
        self.sends, self.recvs = sends, recvs
        self.copies = {}

    def _go(self, src, dst, k, peer):
        copy = send(src, dst, self.sends.at[k], self.recvs.at[k], peer)
        copy.start()
        self.copies[k] = copy

    def start(self):
        for d in (1, 2, 3):
            to = (self.y + d) % 4
            self._go(self.acc.at[to, :, self.first], self.ya.at[d - 1], d - 1, self.peers[d - 1])
        self._go(self.acc.at[:, 1 - self.high, self.second], self.xb, 3, self.partner)

    def middle(self):
        for d in (1, 2, 3):
            self.copies[d - 1].wait_recv()

        def along_y(side):
            total = self.acc[self.y, side, self.first].astype(jnp.float32)
            for d in (0, 1, 2):
                total += self.ya[d, side].astype(jnp.float32)
            return total

        self.xs[...] = along_y(1 - self.high).astype(jnp.bfloat16)
        self._go(self.xs, self.xa, 4, self.partner)
        self.own[0] = along_y(self.high)
        self.copies[3].wait_recv()
        for d in (1, 2, 3):
            to = (self.y + d) % 4
            pair = self.acc[to, self.high, self.second].astype(jnp.float32) + self.xb[to].astype(jnp.float32)
            self.bs[d - 1] = pair.astype(jnp.bfloat16)
            self._go(self.bs.at[d - 1], self.yb.at[d - 1], 4 + d, self.peers[d - 1])
        self.own[1] = self.acc[self.y, self.high, self.second].astype(jnp.float32) + self.xb[self.y].astype(jnp.float32)

    def finish(self):
        self.copies[4].wait_recv()
        first = self.own[0] + self.xa[...].astype(jnp.float32)
        total = self.own[1]
        for d in (1, 2, 3):
            self.copies[4 + d].wait_recv()
            total += self.yb[d - 1].astype(jnp.float32)
        return first, total

    def drain(self):
        for copy in self.copies.values():
            copy.wait_send()


def scatter_buffers(rows, columns):
    return [
        pltpu.VMEM((3, 2, rows, columns), jnp.bfloat16),
        pltpu.VMEM((4, rows, columns), jnp.bfloat16),
        pltpu.VMEM((rows, columns), jnp.bfloat16),
        pltpu.VMEM((rows, columns), jnp.bfloat16),
        pltpu.VMEM((3, rows, columns), jnp.bfloat16),
        pltpu.VMEM((3, rows, columns), jnp.bfloat16),
        pltpu.VMEM((2, rows, columns), jnp.float32),
        pltpu.SemaphoreType.DMA((8,)),
        pltpu.SemaphoreType.DMA((8,)),
    ]


def group_block(ref, rows):
    order = {0: 0, 1: 1, 3: 2, 2: 3}

    def block(r, s, half, view):
        slot = order[(r - view[0]) % 4] * 2 + (s ^ view[1])
        if half is None:
            return ref.at[slot]
        return ref.at[slot, pl.ds(half * (rows // 2), rows // 2)]

    return block


def step_kernel(
    counts_ref, owners_ref, accept_ref, gain_ref, low_hbm, mid_hbm, res_hbm, att_hbm, w_hbm, fc_hbm, target_hbm,
    top_ref, xct_ref, back_ref,
    low, mid, res, att, wbuf, fcw, target,
    psend, prec, acc, gl, gt, attp, resp, ylm, topacc, hits, ranks,
    tsend, trecv, tacc, dsend, drecv, dacc, stat, stats, own_back,
    a0, a1, a2, a3, a4, a5, a6, as_, ar_,
    b0, b1, b2, b3, b4, b5, b6, bs_, br_,
    c0, c1, c2, c3, c4, c5, c6, cs_, cr_,
    d0, d1, d2, d3, d4, d5, d6, ds_, dr_,
    lsem, wsem, psem, qsem, gsend, grecv, hsend, hrecv, tsem, usem, esem, fsem, ssend, srecv, isend, irecv, jsend, jrecv,
    xsem, ksem,
):
    z, xl, y, xh, c = place_in_mesh()
    g, tensor = lax.axis_index("group"), lax.axis_index("tensor")
    bf16, f32 = jnp.bfloat16, jnp.float32
    n_rows, width = att.shape
    half = n_rows // 2
    quarter = half // 2
    columns = fcw.shape[1]
    share = own_back.shape[0]
    compact = 16 * share
    mine_half = compact // 2

    small = [
        pltpu.make_async_copy(src, dst, lsem.at[k])
        for k, (src, dst) in enumerate(
            ((low_hbm, low), (mid_hbm, mid), (att_hbm, att), (res_hbm, res), (target_hbm, target), (fc_hbm, fcw))
        )
    ]
    loads = [
        pltpu.make_async_copy(
            w_hbm.at[:, pl.ds(k * width, width)], wbuf.at[:, pl.ds(k * width, width)], wsem.at[k]
        )
        for k in range(16)
    ]
    for load in (*small[:3], *loads, *small[3:]):
        load.start()
    sib = device(z, xl, y, xh, 1 - c)
    partner = device(z, xl, y, 1 - xh, c)
    peers = [device(z, xl, (y + d) % 4, xh, c) for d in (1, 2, 3)]
    other = device(z, 1 - xl, y, xh, c)
    up, down = device((z + 1) % 4, xl, y, xh, c), device((z + 3) % 4, xl, y, xh, c)
    replicas = [((g + d) % 8, tensor) for d in range(1, 8)]
    enter([sib, partner, *peers, *replicas])

    lane8 = lax.broadcasted_iota(jnp.int32, (n_rows, 8), 1)
    order = accept_ref[...].astype(f32).T
    order = jnp.sum(jnp.where(lane8 == g, order, 0.0), axis=1, keepdims=True).astype(jnp.int32)
    pick = (order == lax.broadcasted_iota(jnp.int32, (n_rows, n_rows), 1)).astype(bf16)

    def picked(ref, rows):
        return jnp.dot(pick[:rows], ref[...], preferred_element_type=f32)

    small[0].wait()
    gl[0, :, :width] = picked(low, half).astype(bf16)
    small[1].wait()
    gl[0, :, width:] = picked(mid, half).astype(bf16)
    lm = RingGather(group_block(gl, half), other, up, down, gsend, grecv)
    top = RingGather(group_block(gt, half), other, up, down, hsend, hrecv)
    lm.own()
    small[2].wait()
    attp[...] = picked(att, n_rows).astype(bf16)
    for load in loads:
        load.wait()

    def to_sibling(r, b):
        rows = pl.ds(r * half, half)
        return send(psend.at[b, rows], prec.at[b, rows], psem.at[r, b], qsem.at[r, b], sib)

    def weight(k):
        return wbuf[:, pl.ds(pl.multiple_of(k * width, width), width)]

    def product(r):
        rows = pl.ds(r * half, half)

        def theirs(b, _):
            part = jnp.dot(attp[rows], weight(2 * b + 1 - c), preferred_element_type=f32)
            psend[b, rows] = part.astype(bf16)
            to_sibling(r, b).start()
            return 0

        lax.fori_loop(0, 8, theirs, 0)

        def ours(b, _):
            part = jnp.dot(attp[rows], weight(2 * b + c), preferred_element_type=f32)
            to_sibling(r, b).wait_recv()
            acc[b // 2, b % 2, rows] = (part + prec[b, rows].astype(f32)).astype(bf16)
            return 0

        lax.fori_loop(0, 8, ours, 0)

    def scatter(into, first, second, bufs, sends, recvs):
        return ChipScatter(into, first, second, y, xh, peers, partner, bufs, sends, recvs)

    product(0)
    rs0 = scatter(acc, pl.ds(0, quarter), pl.ds(quarter, quarter), (a0, a1, a2, a3, a4, a5, a6), as_, ar_)
    rs0.start()
    lm.relay_pair()
    product(1)

    owner = tensor // 2
    position = lax.broadcasted_iota(jnp.int32, (8, n_rows), 1)
    replica = lax.broadcasted_iota(jnp.int32, (8, n_rows), 0)
    limit = jnp.zeros((8, n_rows), jnp.int32)
    for k in range(8):
        limit = jnp.where(replica == k, counts_ref[k], limit)
    hit = jnp.where((owners_ref[...] == owner) & (position < limit), 1.0, 0.0).astype(f32)
    before = lax.broadcasted_iota(jnp.int32, (n_rows, n_rows), 0) < lax.broadcasted_iota(jnp.int32, (n_rows, n_rows), 1)
    hits[...] = hit
    ranks[...] = jnp.dot(hit.astype(bf16), before.astype(bf16), preferred_element_type=f32)

    def offset(which):
        total = jnp.int32(0)
        for k in range(8):
            total += jnp.where(k < which, counts_ref[k], 0)
        return total

    rows_of = []
    for k in range(4):
        which = (tensor % 2) * 4 + k
        member = lax.broadcasted_iota(jnp.int32, (SLOTS, n_rows), 0).astype(f32)
        row = (lax.broadcasted_iota(jnp.int32, (SLOTS, n_rows), 1) + offset(which) + 1).astype(f32)
        here = (ranks[pl.ds(which, 1), :] == member) & (hits[pl.ds(which, 1), :] > 0.5)
        rows_of.append(jnp.sum(jnp.where(here, row, 0.0), axis=1, keepdims=True))
    slot_row = jnp.concatenate(rows_of, axis=0).astype(jnp.int32) - 1
    spread = (slot_row == lax.broadcasted_iota(jnp.int32, (4 * SLOTS, compact), 1)).astype(f32).T.astype(bf16)
    small[4].wait()
    placed = jnp.dot(spread, target[...], preferred_element_type=f32).astype(bf16)
    tacc[...] = placed.reshape(2, 4, 2, share, columns)
    swap_target = send(tacc.at[1 - c], trecv, tsem.at[0], usem.at[0], sib)
    swap_target.start()

    small[3].wait()
    resp[...] = picked(res, n_rows)
    rs0.middle()
    lm.relay_ring(0)
    first, second = rs0.finish()
    first = (resp[:quarter] + first).astype(bf16)
    second = (resp[quarter:half] + second).astype(bf16)
    gt[0, :quarter] = first
    gt[0, quarter:] = second
    top.own()
    top_ref[:quarter] = first
    top_ref[quarter:half] = second
    swap_target.wait_recv()
    tsend[...] = (tacc[c].astype(f32) + trecv[...].astype(f32)).astype(bf16)
    rst = scatter(tsend, pl.ds(0, share // 2), pl.ds(share // 2, share // 2), (c0, c1, c2, c3, c4, c5, c6), cs_, cr_)
    rst.start()
    rs1 = scatter(
        acc, pl.ds(half, quarter), pl.ds(half + quarter, quarter), (b0, b1, b2, b3, b4, b5, b6), bs_, br_
    )
    lm.relay_ring(1)

    for slot in range(8):
        step = (0, 1, 3, 2)[slot // 2]
        which = ((z + step) % 4) * 2 + (xl ^ (slot % 2))
        count = counts_ref[which]
        start = offset(which)
        for part in range(2):
            column = lax.broadcasted_iota(jnp.int32, (mine_half, half), 1)
            row = lax.broadcasted_iota(jnp.int32, (mine_half, half), 0)
            hot = (row + (part * mine_half) - start == column) & (column < count)
            wbuf[:, pl.ds(part * 8 * half + slot * half, half)] = hot.astype(bf16)
    rst.middle()
    rs1.start()
    top.relay_pair()
    lm.last(0)
    lm.last(1)

    hot_width = 8 * half
    held = 2 * hot_width

    def compact_lm(part):
        hot = wbuf[:, pl.ds(part * hot_width, hot_width)]
        for chunk in range(2):
            rows = gl[:, :, chunk * width:(chunk + 1) * width].reshape(hot_width, width)
            got = jnp.dot(hot, rows, preferred_element_type=f32).astype(bf16)
            wbuf[:, pl.ds(held + part * 3 * width + chunk * width, width)] = got

    def product_lm(part):
        rows = wbuf[:, pl.ds(held + part * 3 * width, 2 * width)]
        for chunk in range(2):
            cols = pl.ds(chunk * width, width)
            ylm[part, :, cols] = jnp.dot(rows, fcw[:2 * width, cols], preferred_element_type=f32)

    def turned(part, chunk):
        block = wbuf[:, pl.ds(held + part * 3 * width + chunk * width, width)]
        psend[chunk * 2 + part] = block.T
        copy = pltpu.make_async_copy(
            psend.at[chunk * 2 + part],
            xct_ref.at[pl.ds(chunk * width, width), pl.ds(part * mine_half, mine_half)],
            xsem.at[chunk * 2 + part],
        )
        copy.start()
        return copy

    compact_lm(0)
    top.relay_ring(0)
    compact_lm(1)
    top.relay_ring(1)
    small[5].wait()
    product_lm(0)
    product_lm(1)
    first_t, second_t = rst.finish()
    rs1.middle()

    near = 6 * half

    def top_near(part):
        hot = wbuf[:, pl.ds(part * hot_width, near)]
        topacc[part] = jnp.dot(hot, gt[:6].reshape(near, width), preferred_element_type=f32)

    top_near(0)
    top_near(1)
    top.last(0)
    top.last(1)

    def top_part(part):
        hot = wbuf[:, pl.ds(pl.multiple_of(part * hot_width + near, half), 2 * half)]
        rows = topacc[part] + jnp.dot(hot, gt[6:].reshape(2 * half, width), preferred_element_type=f32)
        rows = rows.astype(bf16)
        wbuf[:, pl.ds(pl.multiple_of(held + part * 3 * width + 2 * width, width), width)] = rows
        return ylm[part] + jnp.dot(rows, fcw[2 * width:], preferred_element_type=f32)

    dsend[...] = top_part(1 - c).astype(bf16)
    swap = send(dsend, drecv, esem.at[0], fsem.at[0], sib)
    swap.start()
    mine = top_part(c)
    swap.wait_recv()
    dacc[...] = (mine + drecv[...].astype(f32)).astype(bf16).reshape(4, 2, share, columns)
    rs2 = scatter(dacc, pl.ds(0, share // 2), pl.ds(share // 2, share // 2), (d0, d1, d2, d3, d4, d5, d6), ds_, dr_)
    rs2.start()

    def sent(b, _):
        to_sibling(0, b).wait_send()
        to_sibling(1, b).wait_send()
        return 0

    lax.fori_loop(0, 8, sent, 0)
    rs2.middle()
    turns = [turned(part, chunk) for part in range(2) for chunk in range(3)]
    first, second = rs2.finish()

    combined = jnp.concatenate([first, second], axis=0)
    wanted = jnp.concatenate([first_t, second_t], axis=0)
    gain = gain_ref[...]
    gained = combined * gain
    lane = lax.broadcasted_iota(jnp.int32, (share, 128), 1)
    sums = jnp.where(
        lane == 0, jnp.sum(combined * combined, axis=1, keepdims=True),
        jnp.where(
            lane == 1, jnp.sum(gained * gained, axis=1, keepdims=True),
            jnp.sum(gained * wanted, axis=1, keepdims=True),
        ),
    )
    stat[...] = jnp.concatenate([sums, jnp.zeros((128 - share, 128), f32)], axis=0).T[:8]
    copies = [send(stat, stats.at[d - 1], ssend.at[d - 1], srecv.at[d - 1], replicas[d - 1]) for d in range(1, 8)]
    for copy in copies:
        copy.start()
    total = stat[...]
    for d in range(7):
        copies[d].wait_recv()
        total += stats[d]
    total = jnp.concatenate([total, jnp.zeros((120, 128), f32)], axis=0).T[:share]
    scale = lax.rsqrt(total[:, 0:1] / D + epsilon)
    weight = 1.0 / offset(8).astype(f32)
    inner = weight * (scale * total[:, 1:2] - total[:, 2:3])
    slope = weight * (gained * scale - wanted)
    own_back[...] = (scale * gain * slope - combined * (scale * scale * scale * inner / D)).astype(bf16)

    def back_at(r, s, part, core):
        chip = ((y + r) % 4) * 2 + (xh + s) % 2
        if part is None:
            return back_ref.at[core, chip]
        return back_ref.at[core, chip, pl.ds(part * (share // 2), share // 2)]

    def back_block(r, s, part, view):
        if (r, s) == (0, 0) and view == (0, 0):
            return own_back
        return back_at(r, s, part, c)

    ag = RingGather(back_block, partner, peers[0], peers[2], isend, irecv)
    ag.own()
    keep = pltpu.make_async_copy(own_back, back_at(0, 0, None, c), ksem.at[0])
    keep.start()
    over = []

    def across(src, ref):
        k = len(over)
        copy = send(src, ref, jsend.at[k], jrecv.at[k], sib)
        copy.start()
        over.append(copy)

    across(own_back, back_at(0, 0, None, c))
    for ref in ag.relay_pair():
        across(ref, ref)
    for flip in (0, 1):
        for ref in ag.relay_ring(flip):
            across(ref, ref)
    for flip in (0, 1):
        for ref in ag.last(flip):
            across(ref, ref)
    first, second = rs1.finish()
    top_ref[half:half + quarter] = (resp[half:half + quarter] + first).astype(bf16)
    top_ref[half + quarter:] = (resp[half + quarter:] + second).astype(bf16)
    landed = [
        (0, 0, None), (0, 1, None), (3, 0, None), (1, 0, None), (3, 1, None), (1, 1, None),
        (2, 0, 0), (2, 0, 1), (2, 1, 0), (2, 1, 1),
    ]
    for k, at in enumerate(landed):
        ref = back_at(*at, 1 - c)
        send(ref, ref, jsend.at[k], jrecv.at[k], sib).wait_recv()
    for copy in (*copies, *over, swap, swap_target):
        copy.wait_send()
    for part in (lm, top, ag, rs0, rs1, rst, rs2):
        part.drain()
    for copy in (*turns, keep):
        copy.wait()


def grad_kernel(accept_ref, top_ref, x_ref, back_ref, top_state_ref, grad_ref):
    g = lax.axis_index("group")
    rows = top_state_ref.shape[0]
    first = pl.program_id(0) * rows
    row = lax.broadcasted_iota(jnp.int32, (rows, top_ref.shape[0]), 0) + first
    put = (accept_ref[pl.ds(g, 1), :] == row).astype(jnp.bfloat16)
    top_state_ref[...] = jnp.dot(put, top_ref[...], preferred_element_type=jnp.float32).astype(jnp.bfloat16)
    grad_ref[...] = jnp.dot(x_ref[...], back_ref[...], preferred_element_type=jnp.float32)


def shards(
    low_state, mid_state, residual, attention, o_weight, fc_weight, norm_gain, target, counts, accept_rows, owners,
):
    rows, width = attention.shape
    half, quarter = rows // 2, rows // 4
    share, columns = target.shape[0] // 2, target.shape[1]
    compact = 16 * share
    vmem = pl.BlockSpec(memory_space=pltpu.VMEM)
    anywhere = pl.BlockSpec(memory_space=pl.ANY)
    dma = pltpu.SemaphoreType.DMA
    bf16, f32 = jnp.bfloat16, jnp.float32
    weights = fc_weight.reshape(3 * width, columns)
    top_perm, turned, back = pl.pallas_call(
        step_kernel,
        out_shape=(
            jax.ShapeDtypeStruct((rows, width), bf16),
            jax.ShapeDtypeStruct((3 * width, compact), bf16),
            jax.ShapeDtypeStruct((2, 8, share, columns), bf16),
        ),
        in_specs=[pl.BlockSpec(memory_space=pltpu.SMEM), vmem, vmem, vmem, *[anywhere] * 7],
        out_specs=(vmem, anywhere, anywhere),
        scratch_shapes=[
            pltpu.VMEM((rows, width), bf16),
            pltpu.VMEM((rows, width), bf16),
            pltpu.VMEM((rows, width), bf16),
            pltpu.VMEM((rows, width), bf16),
            pltpu.VMEM((width, D), bf16),
            pltpu.VMEM((3 * width, columns), bf16),
            pltpu.VMEM((2 * share, columns), bf16),
            pltpu.VMEM((8, rows, width), bf16),
            pltpu.VMEM((8, rows, width), bf16),
            pltpu.VMEM((4, 2, rows, width), bf16),
            pltpu.VMEM((8, half, 2 * width), bf16),
            pltpu.VMEM((8, half, width), bf16),
            pltpu.VMEM((rows, width), bf16),
            pltpu.VMEM((rows, width), f32),
            pltpu.VMEM((2, compact // 2, columns), f32),
            pltpu.VMEM((2, compact // 2, width), f32),
            pltpu.VMEM((8, rows), f32),
            pltpu.VMEM((8, rows), f32),
            pltpu.VMEM((4, 2, share, columns), bf16),
            pltpu.VMEM((4, 2, share, columns), bf16),
            pltpu.VMEM((2, 4, 2, share, columns), bf16),
            pltpu.VMEM((compact // 2, columns), bf16),
            pltpu.VMEM((compact // 2, columns), bf16),
            pltpu.VMEM((4, 2, share, columns), bf16),
            pltpu.VMEM((8, 128), f32),
            pltpu.VMEM((7, 8, 128), f32),
            pltpu.VMEM((share, columns), bf16),
            *scatter_buffers(quarter, width),
            *scatter_buffers(quarter, width),
            *scatter_buffers(share // 2, columns),
            *scatter_buffers(share // 2, columns),
            dma((6,)), dma((16,)), dma((2, 8)), dma((2, 8)), dma((9,)), dma((9,)), dma((9,)), dma((9,)),
            dma((1,)), dma((1,)), dma((1,)), dma((1,)), dma((7,)), dma((7,)), dma((9,)), dma((9,)), dma((10,)), dma((10,)),
            dma((6,)), dma((1,)),
        ],
        compiler_params=pltpu.CompilerParams(collective_id=0, has_side_effects=True, vmem_limit_bytes=62 << 20),
        cost_estimate=pl.CostEstimate(flops=2 * rows * width * D, bytes_accessed=16 << 20, transcendentals=0),
    )(counts, owners, accept_rows, norm_gain[None, :], low_state, mid_state, residual, attention, o_weight, weights, target)
    steps = 4
    top_state, grad = pl.pallas_call(
        grad_kernel,
        grid=(steps,),
        out_shape=(
            jax.ShapeDtypeStruct((rows, width), bf16),
            jax.ShapeDtypeStruct((3 * width, columns), f32),
        ),
        in_specs=[
            pl.BlockSpec((8, rows), lambda i: (0, 0)),
            pl.BlockSpec((rows, width), lambda i: (0, 0)),
            pl.BlockSpec((3 * width // steps, compact), lambda i: (i, 0)),
            pl.BlockSpec((compact, columns), lambda i: (0, 0)),
        ],
        out_specs=(
            pl.BlockSpec((rows // steps, width), lambda i: (i, 0)),
            pl.BlockSpec((3 * width // steps, columns), lambda i: (i, 0)),
        ),
        compiler_params=pltpu.CompilerParams(vmem_limit_bytes=40 << 20),
        cost_estimate=pl.CostEstimate(flops=6 * width * compact * columns, bytes_accessed=12 << 20, transcendentals=0),
    )(accept_rows, top_perm, turned, back.reshape(compact, columns))
    return (top_state, grad.reshape(fc_weight.shape))


def solution(mesh):
    in_specs = (
        P("group", "tensor"),
        P("group", "tensor"),
        P("group", "tensor"),
        P("group", "tensor"),
        P("tensor", None),
        P(None, "tensor", "group"),
        P("group"),
        P("tensor", "group"),
        P(),
        P(),
        P(),
    )
    out_specs = (P("group", "tensor"), P(None, "tensor", "group"))
    return jax.shard_map(shards, mesh=mesh, in_specs=in_specs, out_specs=out_specs, check_vma=False)
```

time: 163 us -> 123 us (0.75)
  matrix products: 13 us -> 0 us
  local copies, waits for them, and re-layouts: 15.8 us -> 4.52 us
  Pallas kernels: 127 us -> 117 us
  other arithmetic: 5.26 us -> 0 us
    dot_general x2 -> x0, matrix products: 13 us -> none  [the longest x1 11.6 us: shards(): lax.dot_general(gathered.reshape(16 * share, 3 * width), back.reshape(16...]
    pallas_call x2, Pallas kernels: 127 us -> 117 us  [the longest x1 112 us: shards(): pl.pallas_call(step_kernel, out_shape=(jax.ShapeDtypeStruct((rows, width)...]
    dot_general x1 -> x0, local copies, waits for them, and re-layouts: 8.67 us -> none  [shards(): lax.dot_general(gathered.reshape(16 * share, 3 * width), back.reshape(16...]
    reduce_sum x6 -> x0, other arithmetic: 3.22 us -> none  [the longest x1 1.29 us: shards(): weight = valid.reshape(share, 1) / jnp.sum(counts).astype(jnp.float32)]
    dynamic_slice x3 -> x0, local copies, waits for them, and re-layouts: 2.72 us -> none  [the longest x1 1.24 us: row_plan(): count = lax.dynamic_index_in_dim(counts, group_index, 0, keepdims=False)]
    unnamed x14 -> x8, local copies, waits for them, and re-layouts: 4.17 us -> 4.52 us
where the time goes in v2:
time: 123 us
  Pallas kernels  117 us (95%)
  local copies, waits for them, and re-layouts  4.52 us (4%)
    pallas_call x1, Pallas kernels, shards(): pl.pallas_call(step_kernel, out_shape=(jax.ShapeDtypeStruct((rows, width)...  112 us
    pallas_call x1, Pallas kernels, shards(): pl.pallas_call(grad_kernel, grid=(steps,), out_shape=(jax.ShapeDtypeStruc...  5.46 us
    unnamed x8, local copies, waits for them, and re-layouts  4.52 us

profile of v2, /device:TPU:1, one launch (start us, length us, event | category | flops | bytes accessed | tf_op | source)
XLA Modules:
  0.0 122.5 jit_solution(18197618782410071496)
XLA Ops:
  0.6 0.0 copy-start
  0.6 111.9 %shard_map.122 = (bf16[512,512]{1,0:T(8,128)(2,1)}, bf16[1536,1024]{1,0:T(8,128)(2,1)}, bf16[2,8,64,1024]{3,2,1,0:T(8,128)(2,1)}) custom-call(s32[8]{0:T(128)} %counts_ref.1, s32[8,512]{1,0:T(8,128)} %owners_ref.1, s32[8,512]{1,0:T(8,128)} %accept_ref.3, f32[1,1024]{1,0:T(1,128)} %bitcast.6, bf16[512,512]{1,0:T(8,128)(2,1)} %low_hbm.1, ...), custom_call_target="tpu_custom_call" | custom-call | flops 4294967296 | bytes 16777216 | tf_op jit(solution)/shard_map/pallas_call | solution.py:507
  112.5 0.0 copy-done
  112.5 0.0 copy-start.1
  112.5 1.6 %copy-done.1 = bf16[2,8,64,1024]{3,2,1,0:T(8,128)(2,1)S(1)} copy-done((bf16[2,8,64,1024]{3,2,1,0:T(8,128)(2,1)S(1)}, bf16[2,8,64,1024]{3,2,1,0:T(8,128)(2,1)}, u32[]{:S(2)}) %copy-start.1) | copy-done | bytes 2097176
  114.1 0.0 copy-start.2
  114.1 1.9 %copy-done.2 = bf16[1536,1024]{1,0:T(8,128)(2,1)S(1)} copy-done((bf16[1536,1024]{1,0:T(8,128)(2,1)S(1)}, bf16[1536,1024]{1,0:T(8,128)(2,1)}, u32[]{:S(2)}) %copy-start.2) | copy-done | bytes 3145752
  116.0 0.0 copy-start.3
  116.0 1.0 copy-done.3
  117.1 5.5 %shard_map.123 = (bf16[512,512]{1,0:T(8,128)(2,1)}, f32[1536,1024]{1,0:T(8,128)}) custom-call(s32[8,512]{1,0:T(8,128)S(1)} %copy-done, bf16[512,512]{1,0:T(8,128)(2,1)S(1)} %copy-done.3, bf16[1536,1024]{1,0:T(8,128)(2,1)S(1)} %copy-done.2, bf16[1024,1024]{1,0:T(8,128)(2,1)S(1)} %bitcast.4), custom_call_target="tpu_custom_call" | custom-call | flops 3221225472 | bytes 12582912 | tf_op jit(solution)/shard_map/pallas_call | solution.py:556
Async XLA Ops:
  0.6 111.9 %copy-start = (s32[8,512]{1,0:T(8,128)S(1)}, s32[8,512]{1,0:T(8,128)}, u32[]{:S(2)}) copy-start(s32[8,512]{1,0:T(8,128)} %accept_ref.3) | copy-start | bytes 49156
  112.5 1.6 %copy-start.1 = (bf16[2,8,64,1024]{3,2,1,0:T(8,128)(2,1)S(1)}, bf16[2,8,64,1024]{3,2,1,0:T(8,128)(2,1)}, u32[]{:S(2)}) copy-start(bf16[2,8,64,1024]{3,2,1,0:T(8,128)(2,1)} %get-tuple-element.9) | copy-start | bytes 6291460
  114.1 1.9 %copy-start.2 = (bf16[1536,1024]{1,0:T(8,128)(2,1)S(1)}, bf16[1536,1024]{1,0:T(8,128)(2,1)}, u32[]{:S(2)}) copy-start(bf16[1536,1024]{1,0:T(8,128)(2,1)} %get-tuple-element.8.x_ref) | copy-start | bytes 9437188
  116.0 1.0 copy-start.3

commit v3 on v2

--- a/solution.py
+++ b/solution.py
@@ -95,17 +95,23 @@
         self.copies[k] = copy
 
     def start(self):
+        self.start_first()
+        self.start_second()
+
+    def start_first(self):
         for d in (1, 2, 3):
             to = (self.y + d) % 4
-            self._go(self.acc.at[to, :, self.first], self.ya.at[d - 1], d - 1, self.peers[d - 1])
-        self._go(self.acc.at[:, 1 - self.high, self.second], self.xb, 3, self.partner)
+            self._go(self.acc.at[(to, slice(None), *self.first)], self.ya.at[d - 1], d - 1, self.peers[d - 1])
+
+    def start_second(self):
+        self._go(self.acc.at[(slice(None), 1 - self.high, *self.second)], self.xb, 3, self.partner)
 
     def middle(self):
         for d in (1, 2, 3):
             self.copies[d - 1].wait_recv()
 
         def along_y(side):
-            total = self.acc[self.y, side, self.first].astype(jnp.float32)
+            total = self.acc[(self.y, side, *self.first)].astype(jnp.float32)
             for d in (0, 1, 2):
                 total += self.ya[d, side].astype(jnp.float32)
             return total
@@ -116,10 +122,10 @@
         self.copies[3].wait_recv()
         for d in (1, 2, 3):
             to = (self.y + d) % 4
-            pair = self.acc[to, self.high, self.second].astype(jnp.float32) + self.xb[to].astype(jnp.float32)
+            pair = self.acc[(to, self.high, *self.second)].astype(jnp.float32) + self.xb[to].astype(jnp.float32)
             self.bs[d - 1] = pair.astype(jnp.bfloat16)
             self._go(self.bs.at[d - 1], self.yb.at[d - 1], 4 + d, self.peers[d - 1])
-        self.own[1] = self.acc[self.y, self.high, self.second].astype(jnp.float32) + self.xb[self.y].astype(jnp.float32)
+        self.own[1] = self.acc[(self.y, self.high, *self.second)].astype(jnp.float32) + self.xb[self.y].astype(jnp.float32)
 
     def finish(self):
         self.copies[4].wait_recv()
@@ -133,6 +139,92 @@
     def drain(self):
         for copy in self.copies.values():
             copy.wait_send()
+
+
+class RingScatter:
+    def __init__(self, acc, halves, rest, y, high, peers, partner, bufs, sends, recvs):
+        self.acc, self.halves, self.rest = acc, halves, rest
+        self.y, self.high, self.peers, self.partner = y, high, peers, partner
+        self.far, self.sums, self.below, self.above, self.xs, self.xa, self.own, self.xb, self.bs, self.yb, self.kept = bufs
+        self.sends, self.recvs = sends, recvs
+        self.copies = {}
+
+    def _go(self, src, dst, k, peer):
+        copy = send(src, dst, self.sends.at[k], self.recvs.at[k], peer)
+        copy.start()
+        self.copies[k] = copy
+
+    def _block(self, step, side, half):
+        return ((self.y + step) % 4, side, *self.halves[half])
+
+    def start(self):
+        both = slice(None)
+        up, down = self.peers[0], self.peers[2]
+        self._go(self.acc.at[self._block(2, both, 0)], self.far.at[0], 0, up)
+        self._go(self.acc.at[self._block(2, both, 1)], self.far.at[1], 1, down)
+        self._go(self.acc.at[(both, 1 - self.high, *self.rest)], self.xb, 4, self.partner)
+        self._go(self.acc.at[self._block(1, both, 1)], self.below.at[1], 2, up)
+        self._go(self.acc.at[self._block(3, both, 0)], self.above.at[0], 3, down)
+
+    def relay(self):
+        for half, step, into, peer in ((0, 1, self.below, self.peers[0]), (1, 3, self.above, self.peers[2])):
+            self.copies[half].wait_recv()
+            for side in (0, 1):
+                total = self.acc[self._block(step, side, half)].astype(jnp.float32) + self.far[half, side].astype(jnp.float32)
+                self.sums[half, side] = total.astype(jnp.bfloat16)
+            self._go(self.sums.at[half], into.at[half], 5 + half, peer)
+        self.copies[4].wait_recv()
+        for d in (1, 2, 3):
+            to = (self.y + d) % 4
+            pair = self.acc[(to, self.high, *self.rest)].astype(jnp.float32) + self.xb[to].astype(jnp.float32)
+            self.bs[d - 1] = pair.astype(jnp.bfloat16)
+            self._go(self.bs.at[d - 1], self.yb.at[d - 1], 7 + d, self.peers[d - 1])
+        self.kept[...] = self.acc[(self.y, self.high, *self.rest)].astype(jnp.float32) + self.xb[self.y].astype(jnp.float32)
+
+    def middle(self):
+        for k in (2, 3, 5, 6):
+            self.copies[k].wait_recv()
+
+        def along_y(side, half):
+            total = self.acc[self._block(0, side, half)].astype(jnp.float32)
+            return total + self.below[half, side].astype(jnp.float32) + self.above[half, side].astype(jnp.float32)
+
+        for half in (0, 1):
+            self.xs[half] = along_y(1 - self.high, half).astype(jnp.bfloat16)
+        self._go(self.xs, self.xa, 7, self.partner)
+        for half in (0, 1):
+            self.own[half] = along_y(self.high, half)
+
+    def finish(self):
+        self.copies[7].wait_recv()
+        rest = self.kept[...]
+        for d in (1, 2, 3):
+            self.copies[7 + d].wait_recv()
+            rest += self.yb[d - 1].astype(jnp.float32)
+        return self.own[0] + self.xa[0].astype(jnp.float32), self.own[1] + self.xa[1].astype(jnp.float32), rest
+
+    def drain(self):
+        for copy in self.copies.values():
+            copy.wait_send()
+
+
+def ring_buffers(half, rest):
+    bf16, f32 = jnp.bfloat16, jnp.float32
+    return [
+        pltpu.VMEM((2, 2, *half), bf16),
+        pltpu.VMEM((2, 2, *half), bf16),
+        pltpu.VMEM((2, 2, *half), bf16),
+        pltpu.VMEM((2, 2, *half), bf16),
+        pltpu.VMEM((2, *half), bf16),
+        pltpu.VMEM((2, *half), bf16),
+        pltpu.VMEM((2, *half), f32),
+        pltpu.VMEM((4, *rest), bf16),
+        pltpu.VMEM((3, *rest), bf16),
+        pltpu.VMEM((3, *rest), bf16),
+        pltpu.VMEM(rest, f32),
+        pltpu.SemaphoreType.DMA((11,)),
+        pltpu.SemaphoreType.DMA((11,)),
+    ]
 
 
 def scatter_buffers(rows, columns):
@@ -165,13 +257,13 @@
     counts_ref, owners_ref, accept_ref, gain_ref, low_hbm, mid_hbm, res_hbm, att_hbm, w_hbm, fc_hbm, target_hbm,
     top_ref, xct_ref, back_ref,
     low, mid, res, att, wbuf, fcw, target,
-    psend, prec, acc, gl, gt, attp, resp, ylm, topacc, hits, ranks,
-    tsend, trecv, tacc, dsend, drecv, dacc, stat, stats, own_back,
-    a0, a1, a2, a3, a4, a5, a6, as_, ar_,
-    b0, b1, b2, b3, b4, b5, b6, bs_, br_,
-    c0, c1, c2, c3, c4, c5, c6, cs_, cr_,
+    psend, prec, acc, gl, gm, gt, attp, resp, ylm, topacc, hits, ranks,
+    tsend, trecv, tacc, dsend, drecv, dacc, stat, stats, own_back, own_wanted,
+    a0, a1, a2, a3, a4, a5, a6, a7, a8, a9, a10, as_, ar_,
+    b0, b1, b2, b3, b4, b5, b6, b7, b8, b9, b10, bs_, br_,
+    c0, c1, c2, c3, c4, c5, c6, c7, c8, c9, c10, cs_, cr_,
     d0, d1, d2, d3, d4, d5, d6, ds_, dr_,
-    lsem, wsem, psem, qsem, gsend, grecv, hsend, hrecv, tsem, usem, esem, fsem, ssend, srecv, isend, irecv, jsend, jrecv,
+    lsem, wsem, psem, qsem, gsend, grecv, msend, mrecv, hsend, hrecv, tsem, usem, esem, fsem, ssend, srecv, isend, irecv, jsend, jrecv,
     xsem, ksem,
 ):
     z, xl, y, xh, c = place_in_mesh()
@@ -179,7 +271,6 @@
     bf16, f32 = jnp.bfloat16, jnp.float32
     n_rows, width = att.shape
     half = n_rows // 2
-    quarter = half // 2
     columns = fcw.shape[1]
     share = own_back.shape[0]
     compact = 16 * share
@@ -215,13 +306,15 @@
     def picked(ref, rows):
         return jnp.dot(pick[:rows], ref[...], preferred_element_type=f32)
 
+    low_part = RingGather(group_block(gl, half), other, up, down, gsend, grecv)
+    mid_part = RingGather(group_block(gm, half), other, up, down, msend, mrecv)
+    top = RingGather(group_block(gt, half), other, up, down, hsend, hrecv)
     small[0].wait()
-    gl[0, :, :width] = picked(low, half).astype(bf16)
+    gl[0] = picked(low, half).astype(bf16)
+    low_part.own()
     small[1].wait()
-    gl[0, :, width:] = picked(mid, half).astype(bf16)
-    lm = RingGather(group_block(gl, half), other, up, down, gsend, grecv)
-    top = RingGather(group_block(gt, half), other, up, down, hsend, hrecv)
-    lm.own()
+    gm[0] = picked(mid, half).astype(bf16)
+    mid_part.own()
     small[2].wait()
     attp[...] = picked(att, n_rows).astype(bf16)
     for load in loads:
@@ -253,14 +346,31 @@
 
         lax.fori_loop(0, 8, ours, 0)
 
-    def scatter(into, first, second, bufs, sends, recvs):
-        return ChipScatter(into, first, second, y, xh, peers, partner, bufs, sends, recvs)
+    cut = 3 * half // 8
+
+    def scatter(into, halves, rest, bufs, sends, recvs):
+        return RingScatter(into, halves, rest, y, xh, peers, partner, bufs, sends, recvs)
+
+    def scatter_rows(r, bufs, sends, recvs):
+        at = r * half
+        return scatter(
+            acc, ((pl.ds(at, cut),), (pl.ds(at + cut, cut),)), (pl.ds(at + 2 * cut, half - 2 * cut),), bufs, sends, recvs
+        )
+
+    def keep_top(r, sums):
+        at = r * half
+        for part in sums:
+            rows = pl.ds(at, part.shape[0])
+            top_ref[rows] = (resp[rows] + part).astype(bf16)
+            at += part.shape[0]
 
     product(0)
-    rs0 = scatter(acc, pl.ds(0, quarter), pl.ds(quarter, quarter), (a0, a1, a2, a3, a4, a5, a6), as_, ar_)
+    rs0 = scatter_rows(0, (a0, a1, a2, a3, a4, a5, a6, a7, a8, a9, a10), as_, ar_)
     rs0.start()
-    lm.relay_pair()
+    low_part.relay_pair()
     product(1)
+    mid_part.relay_pair()
+    low_part.relay_ring(0)
 
     owner = tensor // 2
     position = lax.broadcasted_iota(jnp.int32, (8, n_rows), 1)
@@ -294,26 +404,18 @@
     swap_target = send(tacc.at[1 - c], trecv, tsem.at[0], usem.at[0], sib)
     swap_target.start()
 
+    rs0.relay()
+    low_part.relay_ring(1)
+    mid_part.relay_ring(0)
     small[3].wait()
     resp[...] = picked(res, n_rows)
-    rs0.middle()
-    lm.relay_ring(0)
-    first, second = rs0.finish()
-    first = (resp[:quarter] + first).astype(bf16)
-    second = (resp[quarter:half] + second).astype(bf16)
-    gt[0, :quarter] = first
-    gt[0, quarter:] = second
-    top.own()
-    top_ref[:quarter] = first
-    top_ref[quarter:half] = second
-    swap_target.wait_recv()
-    tsend[...] = (tacc[c].astype(f32) + trecv[...].astype(f32)).astype(bf16)
-    rst = scatter(tsend, pl.ds(0, share // 2), pl.ds(share // 2, share // 2), (c0, c1, c2, c3, c4, c5, c6), cs_, cr_)
-    rst.start()
-    rs1 = scatter(
-        acc, pl.ds(half, quarter), pl.ds(half + quarter, quarter), (b0, b1, b2, b3, b4, b5, b6), bs_, br_
-    )
-    lm.relay_ring(1)
+
+    def sent(b, _):
+        to_sibling(0, b).wait_send()
+        to_sibling(1, b).wait_send()
+        return 0
+
+    lax.fori_loop(0, 8, sent, 0)
 
     for slot in range(8):
         step = (0, 1, 3, 2)[slot // 2]
@@ -325,88 +427,121 @@
             row = lax.broadcasted_iota(jnp.int32, (mine_half, half), 0)
             hot = (row + (part * mine_half) - start == column) & (column < count)
             wbuf[:, pl.ds(part * 8 * half + slot * half, half)] = hot.astype(bf16)
-    rst.middle()
-    rs1.start()
-    top.relay_pair()
-    lm.last(0)
-    lm.last(1)
-
     hot_width = 8 * half
     held = 2 * hot_width
-
-    def compact_lm(part):
-        hot = wbuf[:, pl.ds(part * hot_width, hot_width)]
-        for chunk in range(2):
-            rows = gl[:, :, chunk * width:(chunk + 1) * width].reshape(hot_width, width)
-            got = jnp.dot(hot, rows, preferred_element_type=f32).astype(bf16)
-            wbuf[:, pl.ds(held + part * 3 * width + chunk * width, width)] = got
-
-    def product_lm(part):
-        rows = wbuf[:, pl.ds(held + part * 3 * width, 2 * width)]
-        for chunk in range(2):
-            cols = pl.ds(chunk * width, width)
-            ylm[part, :, cols] = jnp.dot(rows, fcw[:2 * width, cols], preferred_element_type=f32)
-
-    def turned(part, chunk):
-        block = wbuf[:, pl.ds(held + part * 3 * width + chunk * width, width)]
-        psend[chunk * 2 + part] = block.T
-        copy = pltpu.make_async_copy(
-            psend.at[chunk * 2 + part],
-            xct_ref.at[pl.ds(chunk * width, width), pl.ds(part * mine_half, mine_half)],
-            xsem.at[chunk * 2 + part],
-        )
-        copy.start()
-        return copy
-
-    compact_lm(0)
+    near = 6 * half
+
+    def place(part, chunk):
+        return pl.ds(held + part * 3 * width + chunk * width, width)
+
+    def compact_rows(ref, chunk):
+        for part in range(2):
+            hot = wbuf[:, pl.ds(part * hot_width, hot_width)]
+            rows = ref[...].reshape(hot_width, width)
+            wbuf[:, place(part, chunk)] = jnp.dot(hot, rows, preferred_element_type=f32).astype(bf16)
+
+    def product_rows(chunk):
+        for part in range(2):
+            for side in range(2):
+                cols = pl.ds(side * width, width)
+                got = jnp.dot(
+                    wbuf[:, place(part, chunk)], fcw[chunk * width:(chunk + 1) * width, cols], preferred_element_type=f32
+                )
+                ylm[part, :, cols] = got if chunk == 0 else ylm[part, :, cols] + got
+
+    turns = []
+
+    def turn(chunk):
+        for part in range(2):
+            k = chunk * 2 + part
+            psend[k] = wbuf[:, place(part, chunk)].T
+            copy = pltpu.make_async_copy(
+                psend.at[k],
+                xct_ref.at[pl.ds(chunk * width, width), pl.ds(part * mine_half, mine_half)],
+                xsem.at[k],
+            )
+            copy.start()
+            turns.append(copy)
+
+    rs0.middle()
+    swap_target.wait_recv()
+    tsend[...] = (tacc[c].astype(f32) + trecv[...].astype(f32)).astype(bf16)
+    side = 3 * columns // 8
+    every = pl.ds(0, share)
+    rst = scatter(
+        tsend, ((every, pl.ds(0, side)), (every, pl.ds(side, side))), (every, pl.ds(2 * side, columns - 2 * side)),
+        (c0, c1, c2, c3, c4, c5, c6, c7, c8, c9, c10), cs_, cr_,
+    )
+    rst.start()
+    mid_part.relay_ring(1)
+    keep_top(0, rs0.finish())
+    gt[0] = top_ref[:half]
+    top.own()
+    rs1 = scatter_rows(1, (b0, b1, b2, b3, b4, b5, b6, b7, b8, b9, b10), bs_, br_)
+    rs1.start()
+    low_part.last(0)
+    low_part.last(1)
+    compact_rows(gl, 0)
+    rst.relay()
+    small[5].wait()
+    product_rows(0)
+    rst.middle()
+    top.relay_pair()
+    rs1.relay()
+    turn(0)
+    mid_part.last(0)
+    mid_part.last(1)
+    compact_rows(gm, 1)
     top.relay_ring(0)
-    compact_lm(1)
+    product_rows(1)
+    rs1.middle()
+    own_wanted[...] = jnp.concatenate(rst.finish(), axis=1)
+    turn(1)
     top.relay_ring(1)
-    small[5].wait()
-    product_lm(0)
-    product_lm(1)
-    first_t, second_t = rst.finish()
-    rs1.middle()
-
-    near = 6 * half
-
-    def top_near(part):
+    for part in range(2):
         hot = wbuf[:, pl.ds(part * hot_width, near)]
         topacc[part] = jnp.dot(hot, gt[:6].reshape(near, width), preferred_element_type=f32)
-
-    top_near(0)
-    top_near(1)
     top.last(0)
     top.last(1)
 
-    def top_part(part):
+    def swap(side):
+        return send(dsend.at[side], drecv.at[side], esem.at[side], fsem.at[side], sib)
+
+    def top_rows(part):
         hot = wbuf[:, pl.ds(pl.multiple_of(part * hot_width + near, half), 2 * half)]
         rows = topacc[part] + jnp.dot(hot, gt[6:].reshape(2 * half, width), preferred_element_type=f32)
         rows = rows.astype(bf16)
         wbuf[:, pl.ds(pl.multiple_of(held + part * 3 * width + 2 * width, width), width)] = rows
-        return ylm[part] + jnp.dot(rows, fcw[2 * width:], preferred_element_type=f32)
-
-    dsend[...] = top_part(1 - c).astype(bf16)
-    swap = send(dsend, drecv, esem.at[0], fsem.at[0], sib)
-    swap.start()
-    mine = top_part(c)
-    swap.wait_recv()
-    dacc[...] = (mine + drecv[...].astype(f32)).astype(bf16).reshape(4, 2, share, columns)
-    rs2 = scatter(dacc, pl.ds(0, share // 2), pl.ds(share // 2, share // 2), (d0, d1, d2, d3, d4, d5, d6), ds_, dr_)
-    rs2.start()
-
-    def sent(b, _):
-        to_sibling(0, b).wait_send()
-        to_sibling(1, b).wait_send()
-        return 0
-
-    lax.fori_loop(0, 8, sent, 0)
+        return rows
+
+    def features(part, rows, side):
+        cols = pl.ds(side * width, width)
+        return ylm[part, :, cols] + jnp.dot(rows, fcw[2 * width:, cols], preferred_element_type=f32)
+
+    rows = top_rows(1 - c)
+    for side in range(2):
+        dsend[side] = features(1 - c, rows, side).astype(bf16)
+        swap(side).start()
+    rs2 = ChipScatter(
+        dacc, (slice(None), pl.ds(0, width)), (slice(None), pl.ds(width, width)), y, xh, peers, partner,
+        (d0, d1, d2, d3, d4, d5, d6), ds_, dr_,
+    )
+    rows = top_rows(c)
+    for side in range(2):
+        mine = features(c, rows, side)
+        swap(side).wait_recv()
+        both = (mine + drecv[side].astype(f32)).astype(bf16)
+        dacc[:, :, :, pl.ds(side * width, width)] = both.reshape(4, 2, share, width)
+        if side == 0:
+            rs2.start_first()
+        else:
+            rs2.start_second()
     rs2.middle()
-    turns = [turned(part, chunk) for part in range(2) for chunk in range(3)]
+    turn(2)
     first, second = rs2.finish()
 
-    combined = jnp.concatenate([first, second], axis=0)
-    wanted = jnp.concatenate([first_t, second_t], axis=0)
+    combined = jnp.concatenate([first, second], axis=1)
+    wanted = own_wanted[...]
     gain = gain_ref[...]
     gained = combined * gain
     lane = lax.broadcasted_iota(jnp.int32, (share, 128), 1)
@@ -464,9 +599,7 @@
     for flip in (0, 1):
         for ref in ag.last(flip):
             across(ref, ref)
-    first, second = rs1.finish()
-    top_ref[half:half + quarter] = (resp[half:half + quarter] + first).astype(bf16)
-    top_ref[half + quarter:] = (resp[half + quarter:] + second).astype(bf16)
+    keep_top(1, rs1.finish())
     landed = [
         (0, 0, None), (0, 1, None), (3, 0, None), (1, 0, None), (3, 1, None), (1, 1, None),
         (2, 0, 0), (2, 0, 1), (2, 1, 0), (2, 1, 1),
@@ -474,9 +607,9 @@
     for k, at in enumerate(landed):
         ref = back_at(*at, 1 - c)
         send(ref, ref, jsend.at[k], jrecv.at[k], sib).wait_recv()
-    for copy in (*copies, *over, swap, swap_target):
+    for copy in (*copies, *over, swap(0), swap(1), swap_target):
         copy.wait_send()
-    for part in (lm, top, ag, rs0, rs1, rst, rs2):
+    for part in (low_part, mid_part, top, ag, rs0, rs1, rst, rs2):
         part.drain()
     for copy in (*turns, keep):
         copy.wait()
@@ -496,7 +629,7 @@
     low_state, mid_state, residual, attention, o_weight, fc_weight, norm_gain, target, counts, accept_rows, owners,
 ):
     rows, width = attention.shape
-    half, quarter = rows // 2, rows // 4
+    half = rows // 2
     share, columns = target.shape[0] // 2, target.shape[1]
     compact = 16 * share
     vmem = pl.BlockSpec(memory_space=pltpu.VMEM)
@@ -524,7 +657,8 @@
             pltpu.VMEM((8, rows, width), bf16),
             pltpu.VMEM((8, rows, width), bf16),
             pltpu.VMEM((4, 2, rows, width), bf16),
-            pltpu.VMEM((8, half, 2 * width), bf16),
+            pltpu.VMEM((8, half, width), bf16),
+            pltpu.VMEM((8, half, width), bf16),
             pltpu.VMEM((8, half, width), bf16),
             pltpu.VMEM((rows, width), bf16),
             pltpu.VMEM((rows, width), f32),
@@ -535,18 +669,19 @@
             pltpu.VMEM((4, 2, share, columns), bf16),
             pltpu.VMEM((4, 2, share, columns), bf16),
             pltpu.VMEM((2, 4, 2, share, columns), bf16),
-            pltpu.VMEM((compact // 2, columns), bf16),
-            pltpu.VMEM((compact // 2, columns), bf16),
+            pltpu.VMEM((2, compact // 2, width), bf16),
+            pltpu.VMEM((2, compact // 2, width), bf16),
             pltpu.VMEM((4, 2, share, columns), bf16),
             pltpu.VMEM((8, 128), f32),
             pltpu.VMEM((7, 8, 128), f32),
             pltpu.VMEM((share, columns), bf16),
-            *scatter_buffers(quarter, width),
-            *scatter_buffers(quarter, width),
-            *scatter_buffers(share // 2, columns),
-            *scatter_buffers(share // 2, columns),
+            pltpu.VMEM((share, columns), f32),
+            *ring_buffers((3 * half // 8, width), (half // 4, width)),
+            *ring_buffers((3 * half // 8, width), (half // 4, width)),
+            *ring_buffers((share, 3 * columns // 8), (share, columns // 4)),
+            *scatter_buffers(share, columns // 2),
             dma((6,)), dma((16,)), dma((2, 8)), dma((2, 8)), dma((9,)), dma((9,)), dma((9,)), dma((9,)),
-            dma((1,)), dma((1,)), dma((1,)), dma((1,)), dma((7,)), dma((7,)), dma((9,)), dma((9,)), dma((10,)), dma((10,)),
+            dma((9,)), dma((9,)), dma((1,)), dma((1,)), dma((2,)), dma((2,)), dma((7,)), dma((7,)), dma((9,)), dma((9,)), dma((10,)), dma((10,)),
             dma((6,)), dma((1,)),
         ],
         compiler_params=pltpu.CompilerParams(collective_id=0, has_side_effects=True, vmem_limit_bytes=62 << 20),
@@ -570,7 +705,7 @@
             pl.BlockSpec((rows // steps, width), lambda i: (i, 0)),
             pl.BlockSpec((3 * width // steps, columns), lambda i: (i, 0)),
         ),
-        compiler_params=pltpu.CompilerParams(vmem_limit_bytes=40 << 20),
+        compiler_params=pltpu.CompilerParams(vmem_limit_bytes=62 << 20),
         cost_estimate=pl.CostEstimate(flops=6 * width * compact * columns, bytes_accessed=12 << 20, transcendentals=0),
     )(accept_rows, top_perm, turned, back.reshape(compact, columns))
     return (top_state, grad.reshape(fc_weight.shape))

time: 123 us -> 113 us (0.919)
  Pallas kernels: 117 us -> 112 us
  local copies, waits for them, and re-layouts: 4.52 us -> 0 us
    pallas_call x1, Pallas kernels: 112 us -> 104 us  [shards(): pl.pallas_call(step_kernel, out_shape=(jax.ShapeDtypeStruct((rows, width)...]
    unnamed x8 -> x0, local copies, waits for them, and re-layouts: 4.52 us -> none
    pallas_call x1, Pallas kernels: 5.46 us -> 8.15 us  [shards(): pl.pallas_call(grad_kernel, grid=(steps,), out_shape=(jax.ShapeDtypeStruc...]
where the time goes in v3:
time: 113 us
  Pallas kernels  112 us (99%)
    pallas_call x1, Pallas kernels, shards(): pl.pallas_call(step_kernel, out_shape=(jax.ShapeDtypeStruct((rows, width)...  104 us
    pallas_call x1, Pallas kernels, shards(): pl.pallas_call(grad_kernel, grid=(steps,), out_shape=(jax.ShapeDtypeStruc...  8.15 us

profile of v3, /device:TPU:1, one launch (start us, length us, event | category | flops | bytes accessed | tf_op | source)
XLA Modules:
  0.0 113.0 jit_solution(11631040978835373291)
XLA Ops:
  0.6 104.2 %shard_map.122 = (bf16[512,512]{1,0:T(8,128)(2,1)}, bf16[1536,1024]{1,0:T(8,128)(2,1)}, bf16[2,8,64,1024]{3,2,1,0:T(8,128)(2,1)}) custom-call(s32[8]{0:T(128)} %counts_ref.1, s32[8,512]{1,0:T(8,128)} %owners_ref.1, s32[8,512]{1,0:T(8,128)} %accept_ref.3, f32[1,1024]{1,0:T(1,128)} %bitcast.5, bf16[512,512]{1,0:T(8,128)(2,1)} %low_hbm.1, ...), custom_call_target="tpu_custom_call" | custom-call | flops 4294967296 | bytes 16777216 | tf_op jit(solution)/shard_map/pallas_call | solution.py:640
  104.8 8.2 %shard_map.123 = (bf16[512,512]{1,0:T(8,128)(2,1)}, f32[1536,1024]{1,0:T(8,128)}) custom-call(s32[8,512]{1,0:T(8,128)} %accept_ref.3, bf16[512,512]{1,0:T(8,128)(2,1)} %get-tuple-element.7.top_ref, bf16[1536,1024]{1,0:T(8,128)(2,1)} %get-tuple-element.8.x_ref, bf16[1024,1024]{1,0:T(8,128)(2,1)} %bitcast.7), custom_call_target="tpu_custom_call" | custom-call | flops 3221225472 | bytes 12582912 | tf_op jit(solution)/shard_map/pallas_call | solution.py:691

commit v4 on v3

--- a/solution.py
+++ b/solution.py
@@ -19,13 +19,6 @@
 
 def device(z, low, y, high, core):
     return (z * 2 + low, y * 4 + high * 2 + core)
-
-
-def enter(peers):
-    barrier = pltpu.get_barrier_semaphore()
-    for peer in peers:
-        pl.semaphore_signal(barrier, inc=1, device_id=peer, device_id_type=MESH)
-    pl.semaphore_wait(barrier, len(peers))
 
 
 def send(src, dst, send_sem, recv_sem, peer):
@@ -79,6 +72,31 @@
     def drain(self):
         for copy in self.started:
             copy.wait_send()
+
+
+class RingFirstGather(RingGather):
+    def relay_pair(self):
+        return [self._arrived((0, 1, None), 0, self.other)]
+
+    def relay_ring(self, flip):
+        if flip:
+            return [self._arrived((3, 1, None), 3, self.other), self._arrived((1, 1, None), 4, self.other)]
+        low = self._arrived((3, 0, None), 1, self.down)
+        self._go((3, 0, 0), 5, self.up, (1, 0))
+        self._go((3, 0, None), 3, self.other, (0, 1))
+        high = self._arrived((1, 0, None), 2, self.up)
+        self._go((1, 0, 1), 6, self.down, (3, 0))
+        self._go((1, 0, None), 4, self.other, (0, 1))
+        return [low, high]
+
+    def last(self, flip):
+        if flip:
+            return [self._arrived((2, 1, 0), 7, self.other), self._arrived((2, 1, 1), 8, self.other)]
+        first = self._arrived((2, 0, 0), 5, self.down)
+        self._go((2, 0, 0), 7, self.other, (0, 1))
+        second = self._arrived((2, 0, 1), 6, self.up)
+        self._go((2, 0, 1), 8, self.other, (0, 1))
+        return [first, second]
 
 
 class ChipScatter:
@@ -258,12 +276,13 @@
     top_ref, xct_ref, back_ref,
     low, mid, res, att, wbuf, fcw, target,
     psend, prec, acc, gl, gm, gt, attp, resp, ylm, topacc, hits, ranks,
-    tsend, trecv, tacc, dsend, drecv, dacc, stat, stats, own_back, own_wanted,
+    tsend, trecv, tacc, dsend, drecv, dacc, stat, stats, own_back, own_wanted, kept,
     a0, a1, a2, a3, a4, a5, a6, a7, a8, a9, a10, as_, ar_,
     b0, b1, b2, b3, b4, b5, b6, b7, b8, b9, b10, bs_, br_,
     c0, c1, c2, c3, c4, c5, c6, c7, c8, c9, c10, cs_, cr_,
     d0, d1, d2, d3, d4, d5, d6, ds_, dr_,
-    lsem, wsem, psem, qsem, gsend, grecv, msend, mrecv, hsend, hrecv, tsem, usem, esem, fsem, ssend, srecv, isend, irecv, jsend, jrecv,
+    e0, e1, e2, e3, e4, e5, e6, es_, er_,
+    lsem, wsem, psem, qsem, gsend, grecv, msend, mrecv, hsend, hrecv, tsem, usem, esem, fsem, ssend, srecv, isend, irecv, nsend, nrecv, jsend, jrecv,
     xsem, ksem,
 ):
     z, xl, y, xh, c = place_in_mesh()
@@ -288,7 +307,7 @@
         )
         for k in range(16)
     ]
-    for load in (*small[:3], *loads, *small[3:]):
+    for load in small[:2]:
         load.start()
     sib = device(z, xl, y, xh, 1 - c)
     partner = device(z, xl, y, 1 - xh, c)
@@ -296,7 +315,11 @@
     other = device(z, 1 - xl, y, xh, c)
     up, down = device((z + 1) % 4, xl, y, xh, c), device((z + 3) % 4, xl, y, xh, c)
     replicas = [((g + d) % 8, tensor) for d in range(1, 8)]
-    enter([sib, partner, *peers, *replicas])
+    barrier = pltpu.get_barrier_semaphore()
+    for peer in (sib, partner, *peers, *replicas):
+        pl.semaphore_signal(barrier, inc=1, device_id=peer, device_id_type=MESH)
+    for load in (small[2], *loads, *small[3:]):
+        load.start()
 
     lane8 = lax.broadcasted_iota(jnp.int32, (n_rows, 8), 1)
     order = accept_ref[...].astype(f32).T
@@ -311,6 +334,7 @@
     top = RingGather(group_block(gt, half), other, up, down, hsend, hrecv)
     small[0].wait()
     gl[0] = picked(low, half).astype(bf16)
+    pl.semaphore_wait(barrier, 5 + len(replicas))
     low_part.own()
     small[1].wait()
     gm[0] = picked(mid, half).astype(bf16)
@@ -485,8 +509,8 @@
     rst.relay()
     small[5].wait()
     product_rows(0)
+    top.relay_pair()
     rst.middle()
-    top.relay_pair()
     rs1.relay()
     turn(0)
     mid_part.last(0)
@@ -494,13 +518,13 @@
     compact_rows(gm, 1)
     top.relay_ring(0)
     product_rows(1)
-    rs1.middle()
-    own_wanted[...] = jnp.concatenate(rst.finish(), axis=1)
     turn(1)
     top.relay_ring(1)
     for part in range(2):
         hot = wbuf[:, pl.ds(part * hot_width, near)]
         topacc[part] = jnp.dot(hot, gt[:6].reshape(near, width), preferred_element_type=f32)
+    rs1.middle()
+    own_wanted[...] = jnp.concatenate(rst.finish(), axis=1)
     top.last(0)
     top.last(1)
 
@@ -522,96 +546,128 @@
     for side in range(2):
         dsend[side] = features(1 - c, rows, side).astype(bf16)
         swap(side).start()
-    rs2 = ChipScatter(
-        dacc, (slice(None), pl.ds(0, width)), (slice(None), pl.ds(width, width)), y, xh, peers, partner,
-        (d0, d1, d2, d3, d4, d5, d6), ds_, dr_,
-    )
+    piece = share // 2
+    rs2 = [
+        ChipScatter(
+            dacc, (pl.ds(k * piece, piece), pl.ds(0, width)), (pl.ds(k * piece, piece), pl.ds(width, width)),
+            y, xh, peers, partner, bufs, sends, recvs,
+        )
+        for k, (bufs, sends, recvs) in enumerate(
+            (((d0, d1, d2, d3, d4, d5, d6), ds_, dr_), ((e0, e1, e2, e3, e4, e5, e6), es_, er_))
+        )
+    ]
     rows = top_rows(c)
     for side in range(2):
         mine = features(c, rows, side)
         swap(side).wait_recv()
         both = (mine + drecv[side].astype(f32)).astype(bf16)
         dacc[:, :, :, pl.ds(side * width, width)] = both.reshape(4, 2, share, width)
-        if side == 0:
-            rs2.start_first()
-        else:
-            rs2.start_second()
-    rs2.middle()
-    turn(2)
-    first, second = rs2.finish()
-
-    combined = jnp.concatenate([first, second], axis=1)
-    wanted = own_wanted[...]
+        for part in rs2:
+            if side == 0:
+                part.start_first()
+            else:
+                part.start_second()
+    for part in rs2:
+        part.middle()
     gain = gain_ref[...]
-    gained = combined * gain
-    lane = lax.broadcasted_iota(jnp.int32, (share, 128), 1)
-    sums = jnp.where(
-        lane == 0, jnp.sum(combined * combined, axis=1, keepdims=True),
-        jnp.where(
-            lane == 1, jnp.sum(gained * gained, axis=1, keepdims=True),
-            jnp.sum(gained * wanted, axis=1, keepdims=True),
-        ),
-    )
-    stat[...] = jnp.concatenate([sums, jnp.zeros((128 - share, 128), f32)], axis=0).T[:8]
-    copies = [send(stat, stats.at[d - 1], ssend.at[d - 1], srecv.at[d - 1], replicas[d - 1]) for d in range(1, 8)]
-    for copy in copies:
-        copy.start()
-    total = stat[...]
-    for d in range(7):
-        copies[d].wait_recv()
-        total += stats[d]
-    total = jnp.concatenate([total, jnp.zeros((120, 128), f32)], axis=0).T[:share]
-    scale = lax.rsqrt(total[:, 0:1] / D + epsilon)
     weight = 1.0 / offset(8).astype(f32)
-    inner = weight * (scale * total[:, 1:2] - total[:, 2:3])
-    slope = weight * (gained * scale - wanted)
-    own_back[...] = (scale * gain * slope - combined * (scale * scale * scale * inner / D)).astype(bf16)
-
-    def back_at(r, s, part, core):
+    copies = []
+
+    def statistics(k):
+        combined = jnp.concatenate(rs2[k].finish(), axis=1)
+        wanted = own_wanted[k * piece:(k + 1) * piece]
+        gained = combined * gain
+        lane = lax.broadcasted_iota(jnp.int32, (piece, 128), 1)
+        sums = jnp.where(
+            lane == 0, jnp.sum(combined * combined, axis=1, keepdims=True),
+            jnp.where(
+                lane == 1, jnp.sum(gained * gained, axis=1, keepdims=True),
+                jnp.sum(gained * wanted, axis=1, keepdims=True),
+            ),
+        )
+        stat[k] = jnp.concatenate([sums, jnp.zeros((128 - piece, 128), f32)], axis=0).T[:8]
+        for d in range(1, 8):
+            copy = send(stat.at[k], stats.at[k, d - 1], ssend.at[k, d - 1], srecv.at[k, d - 1], replicas[d - 1])
+            copy.start()
+            copies.append(copy)
+        kept[k] = combined
+
+    def backward(k):
+        total = stat[k]
+        for d in range(7):
+            copies[k * 7 + d].wait_recv()
+            total += stats[k, d]
+        total = jnp.concatenate([total, jnp.zeros((120, 128), f32)], axis=0).T[:piece]
+        combined = kept[k]
+        wanted = own_wanted[k * piece:(k + 1) * piece]
+        scale = lax.rsqrt(total[:, 0:1] / D + epsilon)
+        inner = weight * (scale * total[:, 1:2] - total[:, 2:3])
+        slope = weight * (combined * gain * scale - wanted)
+        back = scale * gain * slope - combined * (scale * scale * scale * inner / D)
+        own_back[k * piece:(k + 1) * piece] = back.astype(bf16)
+
+    def back_at(k, r, s, part, core):
         chip = ((y + r) % 4) * 2 + (xh + s) % 2
         if part is None:
-            return back_ref.at[core, chip]
-        return back_ref.at[core, chip, pl.ds(part * (share // 2), share // 2)]
-
-    def back_block(r, s, part, view):
-        if (r, s) == (0, 0) and view == (0, 0):
-            return own_back
-        return back_at(r, s, part, c)
-
-    ag = RingGather(back_block, partner, peers[0], peers[2], isend, irecv)
-    ag.own()
-    keep = pltpu.make_async_copy(own_back, back_at(0, 0, None, c), ksem.at[0])
-    keep.start()
-    over = []
-
-    def across(src, ref):
-        k = len(over)
-        copy = send(src, ref, jsend.at[k], jrecv.at[k], sib)
+            return back_ref.at[core, chip, pl.ds(k * piece, piece)]
+        return back_ref.at[core, chip, pl.ds(k * piece + part * (piece // 2), piece // 2)]
+
+    def own_rows(k):
+        return own_back.at[pl.ds(k * piece, piece)]
+
+    def back_gather(kind, k, sends, recvs):
+        def block(r, s, part, view):
+            if (r, s) == (0, 0) and view == (0, 0):
+                return own_rows(k)
+            return back_at(k, r, s, part, c)
+
+        return kind(block, partner, peers[0], peers[2], sends, recvs)
+
+    ag = [back_gather(RingGather, 0, isend, irecv), back_gather(RingFirstGather, 1, nsend, nrecv)]
+    over = [[], []]
+
+    def across(k, src, ref):
+        n = len(over[k])
+        copy = send(src, ref, jsend.at[k, n], jrecv.at[k, n], sib)
         copy.start()
-        over.append(copy)
-
-    across(own_back, back_at(0, 0, None, c))
-    for ref in ag.relay_pair():
-        across(ref, ref)
+        over[k].append(copy)
+
+    keeps = [
+        pltpu.make_async_copy(own_rows(k), back_at(k, 0, 0, None, c), ksem.at[k]) for k in range(2)
+    ]
+    for k in range(2):
+        statistics(k)
+    for k in range(2):
+        backward(k)
+        ag[k].own()
+        across(k, own_rows(k), back_at(k, 0, 0, None, c))
+        keeps[k].start()
+    for k in range(2):
+        for ref in ag[k].relay_pair():
+            across(k, ref, ref)
     for flip in (0, 1):
-        for ref in ag.relay_ring(flip):
-            across(ref, ref)
+        for k in range(2):
+            for ref in ag[k].relay_ring(flip):
+                across(k, ref, ref)
+    turn(2)
+    keep_top(1, rs1.finish())
     for flip in (0, 1):
-        for ref in ag.last(flip):
-            across(ref, ref)
-    keep_top(1, rs1.finish())
+        for k in range(2):
+            for ref in ag[k].last(flip):
+                across(k, ref, ref)
     landed = [
         (0, 0, None), (0, 1, None), (3, 0, None), (1, 0, None), (3, 1, None), (1, 1, None),
         (2, 0, 0), (2, 0, 1), (2, 1, 0), (2, 1, 1),
     ]
-    for k, at in enumerate(landed):
-        ref = back_at(*at, 1 - c)
-        send(ref, ref, jsend.at[k], jrecv.at[k], sib).wait_recv()
-    for copy in (*copies, *over, swap(0), swap(1), swap_target):
+    for n, at in enumerate(landed):
+        for k in range(2):
+            ref = back_at(k, *at, 1 - c)
+            send(ref, ref, jsend.at[k, n], jrecv.at[k, n], sib).wait_recv()
+    for copy in (*copies, *over[0], *over[1], swap(0), swap(1), swap_target):
         copy.wait_send()
-    for part in (low_part, mid_part, top, ag, rs0, rs1, rst, rs2):
+    for part in (low_part, mid_part, top, *ag, rs0, rs1, rst, *rs2):
         part.drain()
-    for copy in (*turns, keep):
+    for copy in (*turns, *keeps):
         copy.wait()
 
 
@@ -672,17 +728,19 @@
             pltpu.VMEM((2, compact // 2, width), bf16),
             pltpu.VMEM((2, compact // 2, width), bf16),
             pltpu.VMEM((4, 2, share, columns), bf16),
-            pltpu.VMEM((8, 128), f32),
-            pltpu.VMEM((7, 8, 128), f32),
+            pltpu.VMEM((2, 8, 128), f32),
+            pltpu.VMEM((2, 7, 8, 128), f32),
             pltpu.VMEM((share, columns), bf16),
             pltpu.VMEM((share, columns), f32),
+            pltpu.VMEM((2, share // 2, columns), f32),
             *ring_buffers((3 * half // 8, width), (half // 4, width)),
             *ring_buffers((3 * half // 8, width), (half // 4, width)),
             *ring_buffers((share, 3 * columns // 8), (share, columns // 4)),
-            *scatter_buffers(share, columns // 2),
+            *scatter_buffers(share // 2, columns // 2),
+            *scatter_buffers(share // 2, columns // 2),
             dma((6,)), dma((16,)), dma((2, 8)), dma((2, 8)), dma((9,)), dma((9,)), dma((9,)), dma((9,)),
-            dma((9,)), dma((9,)), dma((1,)), dma((1,)), dma((2,)), dma((2,)), dma((7,)), dma((7,)), dma((9,)), dma((9,)), dma((10,)), dma((10,)),
-            dma((6,)), dma((1,)),
+            dma((9,)), dma((9,)), dma((1,)), dma((1,)), dma((2,)), dma((2,)), dma((2, 7)), dma((2, 7)),
+            dma((9,)), dma((9,)), dma((9,)), dma((9,)), dma((2, 10)), dma((2, 10)), dma((6,)), dma((2,)),
         ],
         compiler_params=pltpu.CompilerParams(collective_id=0, has_side_effects=True, vmem_limit_bytes=62 << 20),
         cost_estimate=pl.CostEstimate(flops=2 * rows * width * D, bytes_accessed=16 << 20, transcendentals=0),

time: 113 us -> 110 us (0.973)
  Pallas kernels: 112 us -> 109 us
    pallas_call x1, Pallas kernels: 104 us -> 101 us  [shards(): pl.pallas_call(step_kernel, out_shape=(jax.ShapeDtypeStruct((rows, width)...]
where the time goes in v4:
time: 110 us
  Pallas kernels  109 us (99%)
    pallas_call x1, Pallas kernels, shards(): pl.pallas_call(step_kernel, out_shape=(jax.ShapeDtypeStruct((rows, width)...  101 us
    pallas_call x1, Pallas kernels, shards(): pl.pallas_call(grad_kernel, grid=(steps,), out_shape=(jax.ShapeDtypeStruc...  8.15 us

profile of v4, /device:TPU:1, one launch (start us, length us, event | category | flops | bytes accessed | tf_op | source)
XLA Modules:
  0.0 109.8 jit_solution(1071396035047254482)
XLA Ops:
  0.6 101.0 %shard_map.122 = (bf16[512,512]{1,0:T(8,128)(2,1)}, bf16[1536,1024]{1,0:T(8,128)(2,1)}, bf16[2,8,64,1024]{3,2,1,0:T(8,128)(2,1)}) custom-call(s32[8]{0:T(128)} %counts_ref.1, s32[8,512]{1,0:T(8,128)} %owners_ref.1, s32[8,512]{1,0:T(8,128)} %accept_ref.3, f32[1,1024]{1,0:T(1,128)} %bitcast.5, bf16[512,512]{1,0:T(8,128)(2,1)} %low_hbm.1, ...), custom_call_target="tpu_custom_call" | custom-call | flops 4294967296 | bytes 16777216 | tf_op jit(solution)/shard_map/pallas_call | solution.py:696
  101.7 8.1 %shard_map.123 = (bf16[512,512]{1,0:T(8,128)(2,1)}, f32[1536,1024]{1,0:T(8,128)}) custom-call(s32[8,512]{1,0:T(8,128)} %accept_ref.3, bf16[512,512]{1,0:T(8,128)(2,1)} %get-tuple-element.7.top_ref, bf16[1536,1024]{1,0:T(8,128)(2,1)} %get-tuple-element.8.x_ref, bf16[1024,1024]{1,0:T(8,128)(2,1)} %bitcast.7), custom_call_target="tpu_custom_call" | custom-call | flops 3221225472 | bytes 12582912 | tf_op jit(solution)/shard_map/pallas_call | solution.py:749

commit v5 on v4

--- a/solution.py
+++ b/solution.py
@@ -523,7 +523,6 @@
     for part in range(2):
         hot = wbuf[:, pl.ds(part * hot_width, near)]
         topacc[part] = jnp.dot(hot, gt[:6].reshape(near, width), preferred_element_type=f32)
-    rs1.middle()
     own_wanted[...] = jnp.concatenate(rst.finish(), axis=1)
     top.last(0)
     top.last(1)
@@ -637,6 +636,7 @@
     ]
     for k in range(2):
         statistics(k)
+    rs1.middle()
     for k in range(2):
         backward(k)
         ag[k].own()

time: 110 us -> 112 us (1.018)
  Pallas kernels: 109 us -> 111 us
    pallas_call x1, Pallas kernels: 101 us -> 103 us  [shards(): pl.pallas_call(step_kernel, out_shape=(jax.ShapeDtypeStruct((rows, width)...]
where the time goes in v5:
time: 112 us; the launch traced here: 111 us
  Pallas kernels  111 us (99%)
    pallas_call x1, Pallas kernels, shards(): pl.pallas_call(step_kernel, out_shape=(jax.ShapeDtypeStruct((rows, width)...  103 us
    pallas_call x1, Pallas kernels, shards(): pl.pallas_call(grad_kernel, grid=(steps,), out_shape=(jax.ShapeDtypeStruc...  8.15 us

profile of v5, /device:TPU:1, one launch (start us, length us, event | category | flops | bytes accessed | tf_op | source)
XLA Modules:
  0.0 111.4 jit_solution(9229809011644753051)
XLA Ops:
  0.6 102.7 %shard_map.122 = (bf16[512,512]{1,0:T(8,128)(2,1)}, bf16[1536,1024]{1,0:T(8,128)(2,1)}, bf16[2,8,64,1024]{3,2,1,0:T(8,128)(2,1)}) custom-call(s32[8]{0:T(128)} %counts_ref.1, s32[8,512]{1,0:T(8,128)} %owners_ref.1, s32[8,512]{1,0:T(8,128)} %accept_ref.3, f32[1,1024]{1,0:T(1,128)} %bitcast.5, bf16[512,512]{1,0:T(8,128)(2,1)} %low_hbm.1, ...), custom_call_target="tpu_custom_call" | custom-call | flops 4294967296 | bytes 16777216 | tf_op jit(solution)/shard_map/pallas_call | solution.py:696
  103.3 8.2 %shard_map.123 = (bf16[512,512]{1,0:T(8,128)(2,1)}, f32[1536,1024]{1,0:T(8,128)}) custom-call(s32[8,512]{1,0:T(8,128)} %accept_ref.3, bf16[512,512]{1,0:T(8,128)(2,1)} %get-tuple-element.7.top_ref, bf16[1536,1024]{1,0:T(8,128)(2,1)} %get-tuple-element.8.x_ref, bf16[1024,1024]{1,0:T(8,128)(2,1)} %bitcast.7), custom_call_target="tpu_custom_call" | custom-call | flops 3221225472 | bytes 12582912 | tf_op jit(solution)/shard_map/pallas_call | solution.py:749
